TPU v7x, 256 devices: a whole 4x4x8 slice. The times are simulated.
256 devices in a mesh: pack: 32 (over y, z), hist: 8 (over x, core).
Axes of the slice: x: 4, y: 4, z: 8, core: 2. Of those that a mesh axis runs over, the one named last changes fastest.
Arguments:
- queries: bfloat16 [32, 4096, 2048], P('pack', 'hist'), may hold values from -0.59765625 to 0.59765625
- keys: bfloat16 [32, 4096, 2048], P('pack', 'hist'), may hold values from -6 to 6
- values: bfloat16 [32, 4096, 2048], P('pack', 'hist'), may hold values from -6 to 6
- gates: bfloat16 [32, 4096, 2048], P('pack', 'hist'), may hold values from -6 to 6
- user_ids: int32 [32, 4096], P('pack', 'hist'), may hold values from 0 to 5, never falling along the last dimension, each value on 1 to 1365 neighbouring positions
- forget_rate: float32 [16], replicated, may hold values from 0.0001 to 0.02
- norm_gain: float32 [2048], replicated, may hold values from 0.1 to 1.9
- w_out: bfloat16 [2048, 2048], P('pack'), may hold values from -0.125 to 0.125
Outputs:
- mixed: bfloat16 [32, 4096, 2048], P('pack', 'hist')
Inputs may be any that keep to these rules, and one draw needn't show every extreme that they name: `user_ids`: in each window user ids never fall along the events; each user holds 1 to 1365 consecutive events, and one user exactly 1365.
All inputs are finite; a program needn't handle non-finite values.
Results may differ from a plain program's by a relative error of at most 0.0061.
Values may be sent and summed in bfloat16 or wider, within the bound.
No kernel may reach another device: no remote copies, remote signals or barrier semaphores. Data moves between devices by JAX's collectives and lax.ppermute only.
A program may use at most 128 MiB of HBM per device.

v0:
```python
import jax
import jax.numpy as jnp
from jax import lax
from jax.sharding import PartitionSpec as P

HEADS = 16
GROUP = 128


def passed_along(array, axis, by):
    size = lax.axis_size(axis)
    pairs = [(i, i + by) for i in range(size) if 0 <= i + by < size]
    return lax.ppermute(array, axis, pairs)


def carried_in(array, axis, combine, identity):
    size, here = (lax.axis_size(axis), lax.axis_index(axis))
    everything = jax.tree.map(lambda part: lax.all_gather(part, axis), array)
    start = jax.tree.map(
        lambda part, zero: jnp.broadcast_to(jnp.asarray(zero, part.dtype), part.shape),
        array,
        identity,
    )

    def hop(k, before):
        reached = k < here
        new = combine(before, jax.tree.map(lambda part: part[k], everything))
        return jax.tree.map(lambda a, b: jnp.where(reached, a, b), new, before)

    return lax.fori_loop(0, size, hop, start)


def combine_states(earlier, later):
    return (earlier[0] * later[0], later[0][:, None, None] * earlier[1] + later[1])


def local(queries, keys, values, gates, user_ids, forget_rate, norm_gain, w_out):
    length = queries.shape[1]
    width = queries.shape[2]
    head_dim = width // HEADS
    blocks = length // GROUP
    log_decay = jnp.log1p(-forget_rate)
    users = user_ids[0]
    before = passed_along(users[length - 1 :], "hist", 1)
    prior = jnp.concatenate([before, users[:-1]])
    place_all = jnp.arange(length, dtype=jnp.int32)
    forced = jnp.logical_and(lax.axis_index("hist") == 0, place_all == 0)
    starts = jnp.logical_or(users != prior, forced).astype(jnp.int32)
    seg = users.reshape(blocks, GROUP)
    start_blk = starts.reshape(blocks, GROUP)
    q_blk = queries[0].reshape(blocks, GROUP, HEADS, head_dim)
    k_blk = keys[0].reshape(blocks, GROUP, HEADS, head_dim)
    v_blk = values[0].reshape(blocks, GROUP, HEADS, head_dim)
    place = jnp.arange(GROUP, dtype=jnp.int32)
    diff = place[:, None] - place[None, :]
    causal = diff >= 0
    lag = jnp.where(causal, diff, 0).astype(jnp.float32)
    decay = jnp.exp(lag[None] * log_decay[:, None, None])
    mask = jnp.logical_and(seg[:, :, None] == seg[:, None, :], causal[None])
    scores = jnp.einsum("nthd,nshd->nhts", q_blk, k_blk, preferred_element_type=jnp.float32)
    weights = jnp.where(mask[:, None], scores * decay[None], 0.0).astype(jnp.bfloat16)
    inner = jnp.einsum("nhts,nshd->nthd", weights, v_blk, preferred_element_type=jnp.float32)
    tail = jnp.exp((GROUP - 1 - place).astype(jnp.float32)[None, :] * log_decay[:, None])
    keep_rows = (seg == seg[:, -1:]).astype(jnp.float32)
    scaled = (k_blk * (keep_rows[:, :, None] * tail.T[None])[..., None]).astype(jnp.bfloat16)
    own = jnp.einsum("nshd,nshe->nhde", scaled, v_blk, preferred_element_type=jnp.float32)
    any_start = jnp.max(start_blk, axis=1) > 0
    keep = jnp.where(any_start[:, None], 0.0, jnp.exp(GROUP * log_decay)[None, :])

    def advance(state, item):
        keep_c, own_c = item
        return (keep_c[:, None, None] * state + own_c, state)

    zero_state = jnp.zeros((HEADS, head_dim, head_dim), jnp.float32)
    local_final, local_enter = lax.scan(advance, zero_state, (keep, own))
    keep_before = jnp.cumprod(
        jnp.concatenate([jnp.ones((1, HEADS), jnp.float32), keep[:-1]], axis=0), axis=0
    )
    keep_device = keep_before[-1] * keep[-1]
    identity = (
        jnp.ones((HEADS,), jnp.float32),
        jnp.zeros((HEADS, head_dim, head_dim), jnp.float32),
    )
    incoming = carried_in((keep_device, local_final), "hist", combine_states, identity)[1]
    entering = (local_enter + keep_before[:, :, None, None] * incoming[None]).astype(jnp.bfloat16)
    open_run = (jnp.cumsum(start_blk, axis=1) == 0).astype(jnp.float32)
    reach = jnp.exp((place + 1).astype(jnp.float32)[:, None] * log_decay[None, :])
    factor = open_run[:, :, None] * reach[None]
    carried = (
        jnp.einsum("nthd,nhde->nthe", q_blk, entering, preferred_element_type=jnp.float32)
        * factor[..., None]
    )
    retained = (inner + carried).reshape(length, HEADS, head_dim)
    mean = jnp.mean(retained, axis=2, keepdims=True)
    centred = retained - mean
    variance = jnp.mean(centred * centred, axis=2, keepdims=True)
    normed = (centred * lax.rsqrt(variance + 1e-05)).reshape(length, width) * norm_gain
    gated = (jax.nn.silu(gates[0].astype(jnp.float32)) * normed).astype(jnp.bfloat16)
    mixed = jnp.dot(
        gated, lax.all_gather(w_out, "pack", axis=0, tiled=True), preferred_element_type=jnp.float32
    ).astype(jnp.bfloat16)
    return mixed[None]


def solution(mesh):
    in_specs = (
        P("pack", "hist", None),
        P("pack", "hist", None),
        P("pack", "hist", None),
        P("pack", "hist", None),
        P("pack", "hist"),
        P(),
        P(),
        P("pack", None),
    )
    out_specs = P("pack", "hist", None)
    return jax.shard_map(local, mesh=mesh, in_specs=in_specs, out_specs=out_specs, check_vma=False)
```

profile of v0, /device:TPU:1, one launch (start us, length us, event | category | flops | bytes accessed | tf_op | source)
XLA Modules:
  0.0 219.2 jit_solution(17431535320970974348)
XLA Ops:
  6.5 0.0 all-gather.7.cloned.1.call-start
  6.5 1.2 slice.26
  7.8 4.5 %collective-permute-start = (s32[1]{0:T(128)}, s32[1]{0:T(128)}, u32[]{:S(2)}, u32[]{:S(2)}) collective-permute-start(s32[1]{0:T(128)} %bitcast.4), channel_id=1, source_target_pairs={{0,1},{1,2},{2,3},{3,4},{4,5},{5,6},{6,7},{8,9},{9,10},{10,11},{11... | collective-permute-start | bytes 20 | tf_op jit(solution)/shard_map/ppermute | solution.py:13
  12.3 0.9 slice_reduce_fusion
  13.2 0.8 compare_convert_fusion.1
  13.9 0.7 multiply_exponential_fusion.3
  14.6 3.5 %copy.41 = bf16[64,8,16,128]{3,2,1,0:T(8,128)(2,1)} copy(bf16[64,8,16,128]{3,1,2,0:T(8,128)(2,1)} %bitcast.105) | data formatting | bytes 4194304
  18.1 0.0 copy-start.3
  18.1 3.5 %copy.26 = bf16[4,128,16,128]{1,3,2,0:T(8,128)(2,1)S(1)} copy(bf16[4,128,16,128]{3,2,1,0:T(8,128)(2,1)} %bitcast.100) | data formatting | bytes 4194304 | tf_op jit(solution)/shard_map/reshape;squeeze | solution.py:52
  21.6 0.0 copy-start.1
  21.6 4.3 %copy.42 = bf16[64,8,16,128]{3,2,1,0:T(8,128)(2,1)} copy(bf16[64,8,16,128]{3,1,2,0:T(8,128)(2,1)} %bitcast.106) | data formatting | bytes 4194304
  25.9 0.1 multiply_exponential_fusion.1
  26.0 0.0 collective-permute-done
  26.0 0.0 copy-done.3
  26.0 0.8 fusion.31
  26.8 0.3 reduce_window_sum.11
  27.2 0.1 broadcast_select_fusion
  27.2 4.3 %fusion.10 = f32[4,16,128,128]{3,2,1,0:T(8,128)} fusion(bf16[4,128,16,128]{1,3,2,0:T(8,128)(2,1)S(1)} %copy.26, f32[4,128,16]{1,2,0:T(8,128)S(1)} %get-tuple-element.195, bf16[4,128,16,128]{3,2,1,0:T(8,128)(2,1)} %bitcast.98), kind=kOutput, calls=%fused_computation.25 | convolution fusion | flops 271581184 | bytes 8421376 | tf_op jit(solution)/shard_map/nshd,nshe->nhde/dot_general | solution.py:66
  31.6 0.0 copy-done.1
  31.6 10.0 %while.29 = (s32[]{:T(128)}, f32[16,128,128]{2,1,0:T(8,128)S(1)}, f32[4,16,128,128]{3,2,1,0:T(8,128)}, f32[4,16]{1,0:T(4,128)S(1)}, f32[4,16,128,128]{3,2,1,0:T(8,128)}) while((s32[]{:T(128)}, f32[16,128,128]{2,1,0:T(8,128)S(1)}, f32[4,16,128,128]{3,2,1,0:T(8,128)}, f32[4,16]{1,0:T(4,128)S(1)}, ...), condition=%wide.region_2.3_spmd.clone.clone, body=%wide.region_1.2_spmd.clone.sunk.clone | while | flops 1048579 | bytes 5243664 | solution.py:75
  31.6 1.1 bitcast_dynamic-update-slice_fusion.3
  32.6 1.4 bitcast_add_fusion.4
  34.1 1.1 bitcast_dynamic-update-slice_fusion.3
  35.1 1.4 bitcast_add_fusion.4
  36.6 1.1 bitcast_dynamic-update-slice_fusion.3
  37.7 1.4 bitcast_add_fusion.4
  39.1 1.1 bitcast_dynamic-update-slice_fusion.3
  40.2 1.4 bitcast_add_fusion.4
  41.6 0.0 copy-start
  41.6 1.0 copy-done
  42.6 0.0 all-gather.7.cloned.1.call-update
  42.6 0.0 all-gather.5.cloned.1.call-start
  42.6 0.7 all-gather.5.cloned.1.call-update
  43.4 2.2 %copy.40 = bf16[64,8,16,128]{3,2,1,0:T(8,128)(2,1)S(1)} copy(bf16[64,8,16,128]{3,1,2,0:T(8,128)(2,1)} %bitcast.107) | data formatting | bytes 4194304
  45.6 0.1 compare_and_fusion
  45.8 1.2 multiply_exponential_fusion
  46.9 6.8 %fusion.17 = f32[4,16,128,128]{2,3,1,0:T(8,128)} fusion(bf16[4,128,16,128]{3,2,1,0:T(8,128)(2,1)} %bitcast.99, bf16[4,128,16,128]{1,3,2,0:T(8,128)(2,1)} %copy-done.1, f32[16,128,128]{2,1,0:T(8,128)} %multiply_exponential_fusion, pred[4,128,128]{2,1,0:T(8,128)(4,1)S(1)} %compare_and_fusion, bf16[4,128,16,128]{3,2,1,0:T(8,128)(2,1)S(1)} %bitcast.96), kind=kOutput, calls=%fused_computation.31 | convolution fusion | flops 540016640 | bytes 11599872 | tf_op jit(solution)/shard_map/nhts,nshd->nthd/dot_general | solution.py:62
  53.8 9.5 %all-gather.1 = f32[8,1,16]{2,1,0:T(1,128)S(1)} all-gather(f32[1,1,16]{2,1,0:T(1,128)S(1)} %multiply_bitcast_fusion), channel_id=1, replica_groups=mesh['pack'=32,'hist'=8] {'hist'}, dimensions={0}, use_global_device_ids=true | all-gather | bytes 576 | tf_op jit(solution)/shard_map/all_gather | solution.py:18
  63.3 34.2 %all-gather.7.cloned.1.call-done = f32[128,128,128]{2,1,0:T(8,128)} async-done(((f32[16,128,128]{2,1,0:T(8,128)}), f32[128,128,128]{2,1,0:T(8,128)}) %all-gather.7.cloned.1.call-update) | async-done | bytes 8388624 | tf_op jit(solution)/shard_map/all_gather | solution.py:18
  97.5 11.9 %while.30 = (s32[]{:T(128)}, f32[16,128,128]{2,1,0:T(8,128)S(1)}, s32[]{:T(128)}, f32[8,16]{1,0:T(8,128)S(1)}, f32[8,16,128,128]{3,2,1,0:T(8,128)}) while((s32[]{:T(128)}, f32[16,128,128]{2,1,0:T(8,128)S(1)}, s32[]{:T(128)}, f32[8,16]{1,0:T(8,128)S(1)}, f32[8,16,128,128]{3,2,1,0:T(8,128)}) %tuple.71), condition=%wide.region_5.6_spmd.clone.clone, body=%wide.region_4.5_spmd.clone.sunk.clone | while | flops 1048580 | bytes 3146009 | solution.py:30
  97.5 1.5 fusion.41
  99.0 1.5 fusion.41
  100.5 1.5 fusion.41
  102.0 1.5 fusion.41
  103.5 1.5 fusion.41
  105.0 1.5 fusion.41
  106.5 1.5 fusion.41
  108.0 1.5 fusion.41
  109.5 7.4 %fusion.33 = (f32[4,128,16]{1,2,0:T(8,128)S(1)}, f32[4,128,16,128]{1,3,2,0:T(8,128)}) fusion(f32[4,128,16]{1,2,0:T(8,128)S(1)} %get-tuple-element.194, bf16[4,128,16,128]{3,2,1,0:T(8,128)(2,1)S(1)} %bitcast.97, f32[4,16,128,128]{3,2,1,0:T(8,128)} %get-tuple-element.127, f32[16,128,128]{2,1,0:T(8,128)S(1)} %get-tuple-element.129, ...), kind=kOutput, calls=%fused_computation.66 | convolution fusion | flops 274718720 | bytes 15794432 | tf_op jit(solution)/shard_map/nthd,nhde->nthe/dot_general | solution.py:90
  116.9 0.1 copy.36
  117.0 5.4 %copy.30 = f32[4,128,16,128]{3,2,1,0:T(8,128)} copy(f32[4,128,16,128]{1,3,2,0:T(8,128)} %get-tuple-element.193) | data formatting | bytes 8388608 | tf_op jit(solution)/shard_map/add | solution.py:93
  122.4 3.0 %multiply_reduce_fusion = f32[4,128,16]{1,2,0:T(8,128)S(1)} fusion(f32[4,128,16,128]{1,3,2,0:T(8,128)} %get-tuple-element.193, f32[4,128,16]{1,2,0:T(8,128)S(1)} %broadcast_multiply_fusion), kind=kLoop, calls=%fused_computation.18 | loop fusion | flops 3137536 | bytes 4259840 | tf_op jit(solution)/shard_map/reduce_sum | solution.py:96
  125.5 0.1 copy.37
  125.6 71.4 %all-gather.5.cloned.1.call-done = bf16[2048,2048]{1,0:T(8,128)(2,1)} async-done(((bf16[64,2048]{1,0:T(8,128)(2,1)}), bf16[2048,2048]{1,0:T(8,128)(2,1)}) %all-gather.5.cloned.1.call-update) | async-done | bytes 8388624 | tf_op jit(solution)/shard_map/all_gather | solution.py:100
  197.1 0.0 copy-start.2
  197.1 0.0 copy-start.4
  197.1 0.0 copy-start.5
  197.1 1.1 mul.221
  198.2 1.1 sub.57
  199.3 0.0 copy-done.2
  199.4 0.6 copy-done.4
  199.9 0.0 copy-done.5
  199.9 12.4 %fusion.9 = bf16[1,512,2048]{2,1,0:T(8,128)(2,1)} fusion(bf16[2048,2048]{1,0:T(8,128)(2,1)} %all-gather.5.cloned.1.call-done, f32[64,8,16,128]{3,2,1,0:T(8,128)S(1)} %bitcast.102, f32[64,8,16,128]{3,2,1,0:T(8,128)S(1)} %bitcast.103, f32[64,8,16,128]{3,2,1,0:T(8,128)S(1)} %bitcast.101, bf16[1,512,2048]{2,1,0:T(8,128)(2,1)S(1)} %copy-done.4, ...), kind=kOutput, calls=%fused_computation.24 | convolution fusion | flops 4306501632 | bytes 25174016 | tf_op jit(solution)/shard_map/dot_general | solution.py:99
  (26 shorter events, 0.2 us)
Async XLA Ops:
  6.5 91.0 %all-gather.7.cloned.1.call-start = ((), (), s32[]{:S(2)}) async-start(), calls=%async_computation.1 | async-start | bytes 9437184 | tf_op jit(solution)/shard_map/all_gather | solution.py:18
  7.8 18.2 %collective-permute-start = (s32[1]{0:T(128)}, s32[1]{0:T(128)}, u32[]{:S(2)}, u32[]{:S(2)}) collective-permute-start(s32[1]{0:T(128)} %bitcast.4), channel_id=1, source_target_pairs={{0,1},{1,2},{2,3},{3,4},{4,5},{5,6},{6,7},{8,9},{9,10},{10,11},{11... | collective-permute-start | bytes 20 | tf_op jit(solution)/shard_map/ppermute | solution.py:13
  18.1 7.9 %copy-start.3 = (s32[1,512]{1,0:T(1,128)S(1)}, s32[1,512]{1,0:T(1,128)}, u32[]{:S(2)}) copy-start(s32[1,512]{1,0:T(1,128)} %param.16) | copy-start | bytes 6148
  21.6 10.0 %copy-start.1 = (bf16[4,128,16,128]{1,3,2,0:T(8,128)(2,1)}, bf16[4,128,16,128]{1,3,2,0:T(8,128)(2,1)S(1)}, u32[]{:S(2)}) copy-start(bf16[4,128,16,128]{1,3,2,0:T(8,128)(2,1)S(1)} %copy.26) | copy-start | bytes 6291460
  41.6 1.0 copy-start
  42.6 154.5 %all-gather.5.cloned.1.call-start = ((), (), s32[]{:S(2)}) async-start(), calls=%async_computation | async-start | bytes 8650752 | tf_op jit(solution)/shard_map/all_gather | solution.py:100
  197.1 2.3 %copy-start.2 = (f32[4,128,16,128]{3,2,1,0:T(8,128)S(1)}, f32[4,128,16,128]{3,2,1,0:T(8,128)}, u32[]{:S(2)}) copy-start(f32[4,128,16,128]{3,2,1,0:T(8,128)} %copy.30) | copy-start | bytes 12582916
  197.1 2.9 %copy-start.4 = (bf16[1,512,2048]{2,1,0:T(8,128)(2,1)S(1)}, bf16[1,512,2048]{2,1,0:T(8,128)(2,1)}, u32[]{:S(2)}) copy-start(bf16[1,512,2048]{2,1,0:T(8,128)(2,1)} %param.15) | copy-start | bytes 6291460
  197.1 2.9 %copy-start.5 = (f32[2048]{0:T(1024)S(1)}, f32[2048]{0:T(1024)}, u32[]{:S(2)}) copy-start(f32[2048]{0:T(1024)} %param.18) | copy-start | bytes 24580
Sparse Core Ops, SparseCore 0:
  42.7 54.7 all-gather.6
  100.1 96.9 all-gather.4
where the time goes:
time: 220 us; the launch traced here: 219 us
  waiting for transfers between devices  106 us (48%)
  matrix products  30.9 us (14%)
  other arithmetic  28.8 us (13%)
  local copies, waits for them, and re-layouts  25.2 us (11%)
  between operations  13.6 us (6%)
  blocking collectives  9.47 us (4%)
  starting transfers between devices  4.53 us (2%)
    all_gather x1, waiting for transfers between devices, local(): lax.all_gather(w_out, 'pack', axis=0, tiled=True)  71.4 us
    all_gather x1, waiting for transfers between devices, carried_in(): everything = jax.tree.map(lambda part: lax.all_gather(part, axis), array)  34.2 us
    dot_general x1, matrix products, local(): jnp.dot(gated, lax.all_gather(w_out, 'pack', axis=0, tiled=True), preferr...  12.4 us
    select_n x8, other arithmetic, hop(): return jax.tree.map(lambda a, b: jnp.where(reached, a, b), new, before)  11.7 us
    unnamed x15, local copies, waits for them, and re-layouts  11.6 us
    all_gather x1, blocking collectives, carried_in(): everything = jax.tree.map(lambda part: lax.all_gather(part, axis), array)  9.47 us
    dot_general x1, matrix products, local(): jnp.einsum('nthd,nhde->nthe', q_blk, entering, preferred_element_type=jnp...  7.41 us
    dot_general x1, matrix products, local(): jnp.einsum('nhts,nshd->nthd', weights, v_blk, preferred_element_type=jnp....  6.81 us
  transfers between devices with their start and end apart: 3, of which 2 were waited for; matrix products, arithmetic and copies ran while one was open for 24% of the time, Pallas kernels for 0%

commit v1 on v0

v1 whole, which is shorter than its diff:
```python
import functools

import jax
import jax.numpy as jnp
from jax import lax
from jax.experimental import pallas as pl
from jax.experimental.pallas import tpu as pltpu
from jax.sharding import PartitionSpec as P

HEADS = 16
HEAD = 128
ROWS = 512
HALF = 256
STEP = 4
COLS = STEP * HEAD
WIDTH = 2048
PAYLOAD = WIDTH + 16
NY, NZ, NH = 4, 8, 8
BOTH = ("pack", "hist")
F32 = jnp.float32
BF16 = jnp.bfloat16


def log_decay(rate_ref, h, n=HEAD):
    return jnp.log1p(jnp.full((1, n), -rate_ref[h], F32))


def down_rows(row, rows):
    return jnp.transpose(jnp.broadcast_to(row, (HEAD, rows)))


def state_kernel(rate_ref, u_ref, k_ref, v_ref, pay_ref, mid_ref, mask_ref):
    step = pl.program_id(0)
    u = u_ref[...]

    @pl.when(step == 0)
    def _():
        first, second = u[:, :HALF], u[:, HALF:]
        mask_ref[0] = down_rows((first == u[:, HALF - 1 : HALF]).astype(F32), HALF)
        mask_ref[1] = down_rows((second == u[:, ROWS - 1 :]).astype(F32), HALF)
        pay_ref[WIDTH : WIDTH + 8] = jnp.broadcast_to(u[:, :1].astype(F32), (8, HEAD)).astype(BF16)
        pay_ref[WIDTH + 8 :] = jnp.broadcast_to(u[:, ROWS - 1 :].astype(F32), (8, HEAD)).astype(BF16)

    through = (u[:, HALF - 1 : HALF] == u[:, ROWS - 1 :]).astype(F32)
    left = (HALF - 1 - lax.broadcasted_iota(jnp.int32, (HALF, HEAD), 0)).astype(F32)
    for i in range(STEP):
        ld = log_decay(rate_ref, step * STEP + i)
        tail = jnp.exp(left * ld)
        cols = slice(i * HEAD, (i + 1) * HEAD)
        parts = []
        for b in range(2):
            rows = slice(b * HALF, (b + 1) * HALF)
            scaled = (k_ref[rows, cols].astype(F32) * (mask_ref[b] * tail)).astype(BF16)
            parts.append(
                lax.dot_general(
                    scaled, v_ref[rows, cols], (((0,), (0,)), ((), ())), preferred_element_type=F32
                )
            )
        fade = jnp.exp(jnp.full((1, HEAD), HALF * 1.0, F32) * ld) * through
        mid_ref[i] = parts[0].astype(BF16)
        pay_ref[pl.ds((step * STEP + i) * HEAD, HEAD)] = (parts[1] + fade * parts[0]).astype(BF16)


def inner_kernel(rate_ref, u_ref, q_ref, k_ref, v_ref, mid_ref, out_ref, lag_ref, mask_ref, open_ref):
    step = pl.program_id(0)

    @pl.when(step == 0)
    def _():
        u = u_ref[...]
        t = lax.broadcasted_iota(jnp.int32, (HALF, HALF), 0)
        s = lax.broadcasted_iota(jnp.int32, (HALF, HALF), 1)
        lag_ref[...] = jnp.where(t >= s, t - s, 0).astype(F32)
        for b in range(2):
            across = jnp.broadcast_to(u[:, b * HALF : (b + 1) * HALF], (HALF, HALF))
            down = jnp.transpose(across)
            mask_ref[b] = jnp.where(jnp.logical_and(across == down, t >= s), 1.0, 0.0)
        open_ref[...] = down_rows((u[:, HALF:] == u[:, HALF - 1 : HALF]).astype(F32), HALF)

    past = (1 + lax.broadcasted_iota(jnp.int32, (HALF, HEAD), 0)).astype(F32)
    for i in range(STEP):
        ld = log_decay(rate_ref, step * STEP + i)
        decay = jnp.exp(lag_ref[...] * log_decay(rate_ref, step * STEP + i, HALF))
        cols = slice(i * HEAD, (i + 1) * HEAD)
        for b in range(2):
            rows = slice(b * HALF, (b + 1) * HALF)
            q = q_ref[rows, cols]
            scores = lax.dot_general(
                q, k_ref[rows, cols], (((1,), (1,)), ((), ())), preferred_element_type=F32
            )
            weights = (scores * (decay * mask_ref[b])).astype(BF16)
            inner = jnp.dot(weights, v_ref[rows, cols], preferred_element_type=F32)
            if b == 1:
                carried = jnp.dot(q, mid_ref[i], preferred_element_type=F32)
                inner = inner + carried * (jnp.exp(past * ld) * open_ref[...])
            out_ref[rows, cols] = inner


def pair_kernel(rate_ref, u_ref, own_ref, one_ref, out_ref):
    u = u_ref[...]
    whole = u[:, :1] == u[:, ROWS - 1 :]
    joined = one_ref[WIDTH + 8 : WIDTH + 9].astype(F32) == u[:, :1].astype(F32)
    on = jnp.where(jnp.logical_and(whole, joined), 1.0, 0.0)
    for h in range(HEADS):
        rows = slice(h * HEAD, (h + 1) * HEAD)
        fade = jnp.exp(jnp.full((1, HEAD), ROWS * 1.0, F32) * log_decay(rate_ref, h)) * on
        out_ref[rows] = (own_ref[rows].astype(F32) + fade * one_ref[rows].astype(F32)).astype(BF16)
    out_ref[WIDTH:] = own_ref[WIDTH:]


def gate_kernel(rate_ref, u_ref, one_ref, two_ref, q_ref, part_ref, a_ref, gain_ref, out_ref, open_ref):
    step = pl.program_id(0)
    u = u_ref[...]

    @pl.when(step == 0)
    def _():
        open_ref[...] = down_rows((u == u[:, :1]).astype(F32), ROWS)

    first1 = one_ref[WIDTH : WIDTH + 1].astype(F32)
    last1 = one_ref[WIDTH + 8 : WIDTH + 9].astype(F32)
    last2 = two_ref[WIDTH + 8 : WIDTH + 9].astype(F32)
    near = jnp.where(last1 == u[:, :1].astype(F32), 1.0, 0.0)
    far = jnp.where(jnp.logical_and(first1 == last1, last2 == first1), near, 0.0)
    past = (1 + lax.broadcasted_iota(jnp.int32, (ROWS, HEAD), 0)).astype(F32)
    for i in range(STEP):
        h = step * STEP + i
        ld = log_decay(rate_ref, h)
        cols = slice(i * HEAD, (i + 1) * HEAD)
        rows = pl.ds(pl.multiple_of(h * HEAD, HEAD), HEAD)
        fade = jnp.exp(jnp.full((1, HEAD), ROWS * 1.0, F32) * ld) * far
        state = near * one_ref[rows].astype(F32) + fade * two_ref[rows].astype(F32)
        carried = jnp.dot(q_ref[:, cols], state.astype(BF16), preferred_element_type=F32)
        kept = part_ref[:, cols] + carried * (jnp.exp(past * ld) * open_ref[...])
        mean = jnp.mean(kept, axis=1, keepdims=True)
        centred = kept - mean
        variance = jnp.mean(centred * centred, axis=1, keepdims=True)
        normed = centred * lax.rsqrt(variance + 1e-05) * gain_ref[:, cols]
        a = a_ref[:, cols].astype(F32)
        out_ref[:, cols] = (a / (1.0 + jnp.exp(-a)) * normed).astype(BF16)


def shard_of(way, oc, y, z):
    (y0, z0), (y1, z1) = way
    dy, dz = y0 * (1 - oc) + y1 * oc, z0 * (1 - oc) + z1 * oc
    return ((y + dy + 2 * NY) % NY) * NZ + (z + dz + 2 * NZ) % NZ


def project_kernel(owner, g_ref, *refs):
    pieces, (out_ref, w_ref) = refs[:5], refs[-2:]
    pack = lax.axis_index("pack")
    core = lax.axis_index("hist") % 2
    oc = core if owner == 0 else 1 - core
    y, z = pack // NZ, pack % NZ
    step = pl.program_id(0)

    @pl.when(step == 0)
    def _():
        for piece, ways in zip(pieces, SHARDS):
            for j, way in enumerate(ways):
                rows = pl.ds(pl.multiple_of(shard_of(way, oc, y, z) * 64, 64), 64)
                w_ref[rows] = piece[j * 64 : j * 64 + 64]

    cols = pl.ds(pl.multiple_of(step * 512, 512), 512)
    out_ref[...] = jnp.dot(g_ref[...], w_ref[:, cols], preferred_element_type=F32).astype(BF16)


SMALL = [
    [(0, 0), (0, -4), (-2, 0), (-2, -4), (-1, 0), (-1, -4), (-3, 0), (-3, -4)],
    [(0, 0), (0, -4), (0, -2), (0, 2), (0, -1), (0, -5), (0, -3), (0, 1)],
]


def turned(d):
    return [((y0, z0 + d), (y1 + d, z1)) for (y0, z0), (y1, z1) in zip(*SMALL)]


SHARDS = [turned(0), turned(-1), turned(1), turned(-2)[:4], turned(2)[4:]]


def moves(*ways):
    pairs = []
    for y in range(NY):
        for z in range(NZ):
            for h in range(NH):
                dy, dz = ways[h % 2]
                to = ((y + dy) % NY) * NZ + (z + dz) % NZ
                pairs.append(((y * NZ + z) * NH + h, to * NH + h))
    return pairs


def send(x, *ways):
    return lax.ppermute(x, BOTH, moves(*ways))


def swapped(x):
    return lax.ppermute(x, BOTH, [(i, i ^ 1) for i in range(NY * NZ * NH)])


def gather_first(w):
    core = lax.axis_index("hist") % 2
    x = lax.dynamic_slice_in_dim(w, core * 1024, 1024, 1)
    return x, send(x, (0, 4), (0, 4)), send(x, (2, 0), (0, 2)), send(x, (2, 4), (0, -2))


def gather_second(parts):
    x = jnp.concatenate(parts, 0)
    return x, send(x, (1, 0), (0, 1))


def gather_third(parts):
    x = jnp.concatenate(parts, 0)
    return x, send(x, (0, 1), (1, 0)), send(x, (0, -1), (-1, 0))


def gather_fourth(x, a, b):
    return x, a, b, send(a[:256], (0, 1), (1, 0)), send(b[256:], (0, -1), (-1, 0))


def call(kernel, grid, in_specs, out_specs, out_shape, scratch, flops, nbytes, vmem=14, alias=None):
    return pl.pallas_call(
        kernel,
        grid_spec=pltpu.PrefetchScalarGridSpec(
            num_scalar_prefetch=0,
            grid=grid,
            in_specs=in_specs,
            out_specs=out_specs,
            scratch_shapes=scratch,
        ),
        out_shape=out_shape,
        cost_estimate=pl.CostEstimate(flops=flops, transcendentals=0, bytes_accessed=nbytes),
        compiler_params=pltpu.CompilerParams(vmem_limit_bytes=vmem << 20),
        input_output_aliases=alias or {},
    )


def local(queries, keys, values, gates, user_ids, forget_rate, norm_gain, w_out):
    q, k, v, a = (pltpu.with_memory_space_constraint(x[0], pltpu.HBM) for x in (queries, keys, values, gates))
    gain = norm_gain.reshape(1, WIDTH)
    steps = HEADS // STEP
    smem = pl.BlockSpec(memory_space=pltpu.SMEM)
    users = pl.BlockSpec((1, ROWS), lambda i: (0, 0))
    block = pl.BlockSpec((ROWS, COLS), lambda i: (0, i))
    heads = pl.BlockSpec((STEP, HEAD, HEAD), lambda i: (i, 0, 0))
    full = pl.BlockSpec((PAYLOAD, HEAD), lambda i: (0, 0))
    shape = jax.ShapeDtypeStruct
    pay_shape = shape((PAYLOAD, HEAD), BF16)
    mb = 1 << 20

    first = gather_first(w_out)

    own, mid = call(
        state_kernel, (steps,), [smem, users, block, block], (full, heads),
        (pay_shape, shape((HEADS, HEAD, HEAD), BF16)),
        [pltpu.VMEM((2, HALF, HEAD), F32)], 270 * 10**6, 5 * mb,
    )(forget_rate, user_ids, k, v)
    first, own = lax.optimization_barrier((first, own))
    second = gather_second(first)
    one = lax.ppermute(own, "hist", [(i, i + 1) for i in range(NH - 1)])
    part = call(
        inner_kernel, (steps,), [smem, users, block, block, block, heads], block,
        shape((ROWS, WIDTH), F32),
        [pltpu.VMEM((HALF, HALF), F32), pltpu.VMEM((2, HALF, HALF), F32), pltpu.VMEM((HALF, HEAD), F32)],
        1200 * 10**6, 11 * mb,
    )(forget_rate, user_ids, q, k, v, mid)
    third = gather_third(second)
    pieces = gather_fourth(*third)
    others = [swapped(p) for p in pieces]
    pair = call(
        pair_kernel, (1,), [smem, users, full, full], full, pay_shape, [], 10**6, 3 * mb // 2
    )(forget_rate, user_ids, own, one)
    two = lax.ppermute(pair, "hist", [(i, i + 2) for i in range(NH - 2)])
    gated = call(
        gate_kernel, (steps,),
        [smem, users, full, full, block, block, block, pl.BlockSpec((1, COLS), lambda i: (0, i))],
        block, shape((ROWS, WIDTH), BF16), [pltpu.VMEM((ROWS, HEAD), F32)],
        300 * 10**6, 11 * mb,
    )(forget_rate, user_ids, one, two, q, part, a, gain)

    mixed = None
    for owner, got in enumerate((pieces, others)):

        def column(i, owner=owner):
            core = lax.axis_index("hist") % 2
            return 0, 2 * (core if owner == 0 else 1 - core) + i

        mixed = call(
            functools.partial(project_kernel, owner), (2,),
            [pl.BlockSpec(memory_space=pltpu.VMEM)] * 6 + [pl.BlockSpec(memory_space=pl.ANY)] * owner,
            pl.BlockSpec((ROWS, 512), column), shape((ROWS, WIDTH), BF16),
            [pltpu.VMEM((WIDTH, 1024), BF16)],
            2150 * 10**6, 7 * mb, 14, {6: 0} if owner else None,
        )(gated, *got, *([mixed] if owner else []))
    return mixed[None]


def solution(mesh):
    wide = P("pack", "hist", None)
    in_specs = (wide, wide, wide, wide, P("pack", "hist"), P(), P(), P("pack", None))
    return jax.shard_map(local, mesh=mesh, in_specs=in_specs, out_specs=wide, check_vma=False)
```

time: 220 us -> 84.3 us (0.38)
  waiting for transfers between devices: 106 us -> 6.82 us
  starting transfers between devices: 4.53 us -> 48.6 us
  matrix products: 30.9 us -> 0 us
  other arithmetic: 28.8 us -> 0.03 us
  Pallas kernels: 0 us -> 25.1 us
  local copies, waits for them, and re-layouts: 25.2 us -> 2.45 us
  between operations: 13.6 us -> 0.18 us
  blocking collectives: 9.47 us -> 0 us
    all_gather x2 -> x0, waiting for transfers between devices: 106 us -> none  [the longest x1 71.4 us: local(): lax.all_gather(w_out, 'pack', axis=0, tiled=True)]
    ppermute x1 -> x15, starting transfers between devices: 4.49 us -> 48.6 us  [the longest x8 18.5 us: send(): return lax.ppermute(x, BOTH, moves(*ways))]
    dot_general x4 -> x0, matrix products: 30.9 us -> none  [the longest x1 12.4 us: local(): jnp.dot(gated, lax.all_gather(w_out, 'pack', axis=0, tiled=True), preferr...]
    pallas_call x0 -> x6, Pallas kernels: none -> 25.1 us  [the longest x2 7.53 us: local(): call(functools.partial(project_kernel, owner), (2,), [pl.BlockSpec(memory...]
    select_n x9 -> x0, other arithmetic: 11.7 us -> none  [the longest x8 11.7 us: hop(): return jax.tree.map(lambda a, b: jnp.where(reached, a, b), new, before)]
    all_gather x1 -> x0, blocking collectives: 9.47 us -> none  [carried_in(): everything = jax.tree.map(lambda part: lax.all_gather(part, axis), array)]
    unnamed x15 -> x12, local copies, waits for them, and re-layouts: 11.6 us -> 2.33 us
    ppermute x1 -> x15, waiting for transfers between devices: 0.01 us -> 6.82 us  [the longest x8 5.08 us: send(): return lax.ppermute(x, BOTH, moves(*ways))]
  transfers between devices with their start and end apart: 3 -> 15, of which waited for: 2 -> 4; matrix products, arithmetic and copies ran while one was open for 24% -> 0% of each run, Pallas kernels for 0% -> 26%
where the time goes in v1:
time: 84.3 us; the launch traced here: 83.3 us
  starting transfers between devices  48.6 us (58%)
  Pallas kernels  25.1 us (30%)
  waiting for transfers between devices  6.82 us (8%)
  local copies, waits for them, and re-layouts  2.45 us (3%)
    ppermute x8, starting transfers between devices, send(): return lax.ppermute(x, BOTH, moves(*ways))  18.5 us
    ppermute x5, starting transfers between devices, swapped(): return lax.ppermute(x, BOTH, [(i, i ^ 1) for i in range(NY * NZ * NH)])  18.5 us
    ppermute x1, starting transfers between devices, local(): one = lax.ppermute(own, 'hist', [(i, i + 1) for i in range(NH - 1)])  8.5 us
    pallas_call x2, Pallas kernels, local(): call(functools.partial(project_kernel, owner), (2,), [pl.BlockSpec(memory...  7.53 us
    pallas_call x1, Pallas kernels, local(): call(inner_kernel, (steps,), [smem, users, block, block, block, heads], b...  6.58 us
    pallas_call x1, Pallas kernels, local(): call(gate_kernel, (steps,), [smem, users, full, full, block, block, block...  6.15 us
    ppermute x8, waiting for transfers between devices, send(): return lax.ppermute(x, BOTH, moves(*ways))  5.08 us
    pallas_call x1, Pallas kernels, local(): call(state_kernel, (steps,), [smem, users, block, block], (full, heads),...  4.01 us
  transfers between devices with their start and end apart: 15, of which 4 were waited for; matrix products, arithmetic and copies ran while one was open for 0% of the time, Pallas kernels for 26%

profile of v1, /device:TPU:1, one launch (start us, length us, event | category | flops | bytes accessed | tf_op | source)
XLA Modules:
  0.0 83.3 jit_solution(17029818726436757889)
XLA Ops:
  0.0 0.0 copy-start
  0.0 0.9 %copy-done = bf16[64,2048]{1,0:T(8,128)(2,1)S(1)} copy-done((bf16[64,2048]{1,0:T(8,128)(2,1)S(1)}, bf16[64,2048]{1,0:T(8,128)(2,1)}, u32[]{:S(2)}) %copy-start) | copy-done | bytes 262168
  1.0 7.8 %collective-permute-start = (bf16[64,1024]{1,0:T(8,128)(2,1)S(1)}, bf16[64,1024]{1,0:T(8,128)(2,1)S(1)}, u32[]{:S(2)}, u32[]{:S(2)}) collective-permute-start(bf16[64,1024]{1,0:T(8,128)(2,1)S(1)} %constant_dynamic-slice_fusion), channel_id=1, source_target_pairs={{0,32},{1,33},{2,34},{3,35},{4,36},{5,37},{6,38},{7,39},{8,40},{9,... | collective-permute-start | bytes 393224 | tf_op jit(solution)/shard_map/ppermute | solution.py:191
  8.8 1.2 %collective-permute-start.1 = (bf16[64,1024]{1,0:T(8,128)(2,1)S(1)}, bf16[64,1024]{1,0:T(8,128)(2,1)S(1)}, u32[]{:S(2)}, u32[]{:S(2)}) collective-permute-start(bf16[64,1024]{1,0:T(8,128)(2,1)S(1)} %constant_dynamic-slice_fusion), channel_id=1, source_target_pairs={{0,128},{1,17},{2,130},{3,19},{4,132},{5,21},{6,134},{7,23},{8,136... | collective-permute-start | bytes 393224 | tf_op jit(solution)/shard_map/ppermute | solution.py:191
  10.0 2.4 %collective-permute-start.2 = (bf16[64,1024]{1,0:T(8,128)(2,1)S(1)}, bf16[64,1024]{1,0:T(8,128)(2,1)S(1)}, u32[]{:S(2)}, u32[]{:S(2)}) collective-permute-start(bf16[64,1024]{1,0:T(8,128)(2,1)S(1)} %constant_dynamic-slice_fusion), channel_id=1, source_target_pairs={{0,160},{1,49},{2,162},{3,51},{4,164},{5,53},{6,166},{7,55},{8,168... | collective-permute-start | bytes 393224 | tf_op jit(solution)/shard_map/ppermute | solution.py:191
  12.4 0.0 copy-start.1
  12.4 0.7 copy-done.1
  13.0 0.0 copy-start.3
  13.0 0.7 copy-done.3
  13.7 4.0 %shard_map.82 = (bf16[2064,128]{1,0:T(8,128)(2,1)S(1)}, bf16[16,128,128]{2,1,0:T(8,128)(2,1)S(1)}) custom-call(f32[16]{0:T(128)S(1)} %copy-done.3, s32[1,512]{1,0:T(1,128)S(1)} %copy-done.1, bf16[512,2048]{1,0:T(8,128)(2,1)} %bitcast.9, bf16[512,2048]{1,0:T(8,128)(2,1)} %bitcast.11), custom_call_target="tpu_custom_call" | custom-call | flops 270000000 | bytes 5242880 | tf_op jit(solution)/shard_map/pallas_call | solution.py:250
  17.7 0.0 collective-permute-done
  17.7 0.0 collective-permute-done.1
  17.7 1.1 %collective-permute-done.2 = bf16[64,1024]{1,0:T(8,128)(2,1)S(1)} collective-permute-done((bf16[64,1024]{1,0:T(8,128)(2,1)S(1)}, bf16[64,1024]{1,0:T(8,128)(2,1)S(1)}, u32[]{:S(2)}, u32[]{:S(2)}) %collective-permute-start.2) | collective-permute-done | bytes 131104 | tf_op jit(solution)/shard_map/ppermute | solution.py:191
  18.9 1.6 %collective-permute-start.5 = (bf16[256,1024]{1,0:T(8,128)(2,1)S(1)}, bf16[256,1024]{1,0:T(8,128)(2,1)S(1)}, u32[]{:S(2)}, u32[]{:S(2)}) collective-permute-start(bf16[256,1024]{1,0:T(8,128)(2,1)S(1)} %pad_maximum_fusion), channel_id=1, source_target_pairs={{0,64},{1,9},{2,66},{3,11},{4,68},{5,13},{6,70},{7,15},{8,72},{9,1... | collective-permute-start | bytes 1572872 | tf_op jit(solution)/shard_map/ppermute | solution.py:191
  20.4 8.5 %collective-permute-start.3 = (bf16[2064,128]{1,0:T(8,128)(2,1)S(1)}, bf16[2064,128]{1,0:T(8,128)(2,1)S(1)}, u32[]{:S(2)}, u32[]{:S(2)}) collective-permute-start(bf16[2064,128]{1,0:T(8,128)(2,1)S(1)} %get-tuple-element.13.own_ref), channel_id=1, source_target_pairs={{0,1},{1,2},{2,3},{3,4},{4,5},{5,6},{6,7},{8,9},{9,10},{10,11},{11... | collective-permute-start | bytes 1585160 | tf_op jit(solution)/shard_map/ppermute | solution.py:257
  29.0 1.5 %collective-permute-done.5 = bf16[256,1024]{1,0:T(8,128)(2,1)S(1)} collective-permute-done((bf16[256,1024]{1,0:T(8,128)(2,1)S(1)}, bf16[256,1024]{1,0:T(8,128)(2,1)S(1)}, u32[]{:S(2)}, u32[]{:S(2)}) %collective-permute-start.5) | collective-permute-done | bytes 524320 | tf_op jit(solution)/shard_map/ppermute | solution.py:191
  30.6 1.1 %collective-permute-start.7 = (bf16[512,1024]{1,0:T(8,128)(2,1)S(1)}, bf16[512,1024]{1,0:T(8,128)(2,1)S(1)}, u32[]{:S(2)}, u32[]{:S(2)}) collective-permute-start(bf16[512,1024]{1,0:T(8,128)(2,1)S(1)} %constant_dynamic-update-slice_fusion.refs_0_), channel_id=1, source_target_pairs={{0,8},{1,65},{2,10},{3,67},{4,12},{5,69},{6,14},{7,71},{8,16},{9,7... | collective-permute-start | bytes 3145736 | tf_op jit(solution)/shard_map/ppermute | solution.py:191
  31.7 1.7 %collective-permute-start.9 = (bf16[512,1024]{1,0:T(8,128)(2,1)S(1)}, bf16[512,1024]{1,0:T(8,128)(2,1)S(1)}, u32[]{:S(2)}, u32[]{:S(2)}) collective-permute-start(bf16[512,1024]{1,0:T(8,128)(2,1)S(1)} %constant_dynamic-update-slice_fusion.refs_0_), channel_id=1, source_target_pairs={{0,56},{1,193},{2,58},{3,195},{4,60},{5,197},{6,62},{7,199},{8,0},... | collective-permute-start | bytes 3145736 | tf_op jit(solution)/shard_map/ppermute | solution.py:191
  33.3 1.7 %collective-permute-done.3.one_ref = bf16[2064,128]{1,0:T(8,128)(2,1)S(1)} collective-permute-done((bf16[2064,128]{1,0:T(8,128)(2,1)S(1)}, bf16[2064,128]{1,0:T(8,128)(2,1)S(1)}, u32[]{:S(2)}, u32[]{:S(2)}) %collective-permute-start.3) | collective-permute-done | bytes 528416 | tf_op jit(solution)/shard_map/ppermute | solution.py:257
  35.1 0.9 %shard_map.83 = bf16[2064,128]{1,0:T(8,128)(2,1)S(1)} custom-call(f32[16]{0:T(128)S(1)} %copy-done.3, s32[1,512]{1,0:T(1,128)S(1)} %copy-done.1, bf16[2064,128]{1,0:T(8,128)(2,1)S(1)} %get-tuple-element.13.own_ref, bf16[2064,128]{1,0:T(8,128)(2,1)S(1)} %collective-permute-done.3.one_ref), custom_call_target="tpu_custom_call" | custom-call | flops 1000000 | bytes 1572864 | tf_op jit(solution)/shard_map/pallas_call | solution.py:267
  35.9 3.1 %collective-permute-start.4 = (bf16[2064,128]{1,0:T(8,128)(2,1)S(1)}, bf16[2064,128]{1,0:T(8,128)(2,1)S(1)}, u32[]{:S(2)}, u32[]{:S(2)}) collective-permute-start(bf16[2064,128]{1,0:T(8,128)(2,1)S(1)} %shard_map.83), channel_id=1, source_target_pairs={{0,2},{1,3},{2,4},{3,5},{4,6},{5,7},{8,10},{9,11},{10,12},{11,13},... | collective-permute-start | bytes 1585160 | tf_op jit(solution)/shard_map/ppermute | solution.py:270
  39.1 4.9 %collective-permute-start.6 = (bf16[512,1024]{1,0:T(8,128)(2,1)S(1)}, bf16[512,1024]{1,0:T(8,128)(2,1)S(1)}, u32[]{:S(2)}, u32[]{:S(2)}) collective-permute-start(bf16[512,1024]{1,0:T(8,128)(2,1)S(1)} %constant_dynamic-update-slice_fusion.refs_0_), channel_id=1, source_target_pairs={{0,1},{1,0},{2,3},{3,2},{4,5},{5,4},{6,7},{7,6},{8,9},{9,8},{10,11... | collective-permute-start | bytes 3145736 | tf_op jit(solution)/shard_map/ppermute | solution.py:195
  44.0 2.4 %collective-permute-done.7.refs_1_ = bf16[512,1024]{1,0:T(8,128)(2,1)S(1)} collective-permute-done((bf16[512,1024]{1,0:T(8,128)(2,1)S(1)}, bf16[512,1024]{1,0:T(8,128)(2,1)S(1)}, u32[]{:S(2)}, u32[]{:S(2)}) %collective-permute-start.7) | collective-permute-done | bytes 1048608 | tf_op jit(solution)/shard_map/ppermute | solution.py:191
  46.5 0.1 collective-permute-start.11
  46.6 0.0 collective-permute-done.9.refs_2_
  46.7 2.7 %collective-permute-start.13 = (bf16[256,1024]{1,0:T(8,128)(2,1)S(1)}, bf16[256,1024]{1,0:T(8,128)(2,1)S(1)}, u32[]{:S(2)}, u32[]{:S(2)}) collective-permute-start(bf16[256,1024]{1,0:T(8,128)(2,1)S(1)} %slice.9), channel_id=1, source_target_pairs={{0,56},{1,193},{2,58},{3,195},{4,60},{5,197},{6,62},{7,199},{8,0},... | collective-permute-start | bytes 1572872 | tf_op jit(solution)/shard_map/ppermute | solution.py:191
  49.4 6.5 %collective-permute-start.10 = (bf16[512,1024]{1,0:T(8,128)(2,1)S(1)}, bf16[512,1024]{1,0:T(8,128)(2,1)S(1)}, u32[]{:S(2)}, u32[]{:S(2)}) collective-permute-start(bf16[512,1024]{1,0:T(8,128)(2,1)S(1)} %collective-permute-done.9.refs_2_), channel_id=1, source_target_pairs={{0,1},{1,0},{2,3},{3,2},{4,5},{5,4},{6,7},{7,6},{8,9},{9,8},{10,11... | collective-permute-start | bytes 3145736 | tf_op jit(solution)/shard_map/ppermute | solution.py:195
  55.9 0.0 collective-permute-done.4.two_ref
  55.9 0.0 collective-permute-start.8
  55.9 0.0 collective-permute-done.11.refs_3_
  55.9 7.0 %collective-permute-start.12 = (bf16[256,1024]{1,0:T(8,128)(2,1)S(1)}, bf16[256,1024]{1,0:T(8,128)(2,1)S(1)}, u32[]{:S(2)}, u32[]{:S(2)}) collective-permute-start(bf16[256,1024]{1,0:T(8,128)(2,1)S(1)} %collective-permute-done.11.refs_3_), channel_id=1, source_target_pairs={{0,1},{1,0},{2,3},{3,2},{4,5},{5,4},{6,7},{7,6},{8,9},{9,8},{10,11... | collective-permute-start | bytes 1572872 | tf_op jit(solution)/shard_map/ppermute | solution.py:195
  62.9 0.0 collective-permute-done.13.refs_4_
  62.9 0.0 collective-permute-start.14
  62.9 0.0 copy-start.2
  62.9 6.6 %shard_map.84.part_ref = f32[512,2048]{1,0:T(8,128)S(1)} custom-call(f32[16]{0:T(128)S(1)} %copy-done.3, s32[1,512]{1,0:T(1,128)S(1)} %copy-done.1, bf16[512,2048]{1,0:T(8,128)(2,1)} %bitcast.7, bf16[512,2048]{1,0:T(8,128)(2,1)} %bitcast.10, bf16[512,2048]{1,0:T(8,128)(2,1)} %bitcast.12, bf16[16,128,128]{2,1,0:T(8,128)(2,1)S(1)} %get-tuple-element.14.mid_ref), custom_call_target="tpu_custom_call" | custom-call | flops 1200000000 | bytes 11534336 | tf_op jit(solution)/shard_map/pallas_call | solution.py:258
  69.5 0.0 copy-done.2
  69.5 6.1 %shard_map.85.g_ref = bf16[512,2048]{1,0:T(8,128)(2,1)S(1)} custom-call(f32[16]{0:T(128)S(1)} %copy-done.3, s32[1,512]{1,0:T(1,128)S(1)} %copy-done.1, bf16[2064,128]{1,0:T(8,128)(2,1)S(1)} %collective-permute-done.3.one_ref, bf16[2064,128]{1,0:T(8,128)(2,1)S(1)} %collective-permute-done.4.two_ref, bf16[512,2048]{1,0:T(8,128)(2,1)} %bitcast.8, ...), custom_call_target="tpu_custom_call" | custom-call | flops 300000000 | bytes 11534336 | tf_op jit(solution)/shard_map/pallas_call | solution.py:271
  75.7 3.8 %shard_map.86.refs_5_ = bf16[512,2048]{1,0:T(8,128)(2,1)} custom-call(bf16[512,2048]{1,0:T(8,128)(2,1)S(1)} %shard_map.85.g_ref, bf16[512,1024]{1,0:T(8,128)(2,1)S(1)} %constant_dynamic-update-slice_fusion.refs_0_, bf16[512,1024]{1,0:T(8,128)(2,1)S(1)} %collective-permute-done.7.refs_1_, bf16[512,1024]{1,0:T(8,128)(2,1)S(1)} %collective-permute-done.9.refs_2_, ...), custom_call_target="tpu_custom_call" | custom-call | flops 2150000128 | bytes 7340032 | tf_op jit(solution)/shard_map/pallas_call | solution.py:285
  79.5 0.0 collective-permute-done.6.refs_0_
  79.5 0.0 collective-permute-done.12.refs_3_
  79.5 0.0 collective-permute-done.14.refs_4_
  79.5 0.0 collective-permute-done.10.refs_2_
  79.5 0.0 collective-permute-done.8.refs_1_
  79.5 3.8 %shard_map.87 = bf16[512,2048]{1,0:T(8,128)(2,1)} custom-call(bf16[512,2048]{1,0:T(8,128)(2,1)S(1)} %shard_map.85.g_ref, bf16[512,1024]{1,0:T(8,128)(2,1)S(1)} %collective-permute-done.6.refs_0_, bf16[512,1024]{1,0:T(8,128)(2,1)S(1)} %collective-permute-done.8.refs_1_, ...), custom_call_target="tpu_custom_call", output_to_operand_aliasing={{}: (6, {})} | custom-call | flops 2150000128 | bytes 7340032 | tf_op jit(solution)/shard_map/pallas_call | solution.py:285
  (9 shorter events, 0.2 us)
Async XLA Ops:
  0.0 1.0 %copy-start = (bf16[64,2048]{1,0:T(8,128)(2,1)S(1)}, bf16[64,2048]{1,0:T(8,128)(2,1)}, u32[]{:S(2)}) copy-start(bf16[64,2048]{1,0:T(8,128)(2,1)} %param.15) | copy-start | bytes 786436
  1.0 16.8 %collective-permute-start = (bf16[64,1024]{1,0:T(8,128)(2,1)S(1)}, bf16[64,1024]{1,0:T(8,128)(2,1)S(1)}, u32[]{:S(2)}, u32[]{:S(2)}) collective-permute-start(bf16[64,1024]{1,0:T(8,128)(2,1)S(1)} %constant_dynamic-slice_fusion), channel_id=1, source_target_pairs={{0,32},{1,33},{2,34},{3,35},{4,36},{5,37},{6,38},{7,39},{8,40},{9,... | collective-permute-start | bytes 393224 | tf_op jit(solution)/shard_map/ppermute | solution.py:191
  8.8 8.9 %collective-permute-start.1 = (bf16[64,1024]{1,0:T(8,128)(2,1)S(1)}, bf16[64,1024]{1,0:T(8,128)(2,1)S(1)}, u32[]{:S(2)}, u32[]{:S(2)}) collective-permute-start(bf16[64,1024]{1,0:T(8,128)(2,1)S(1)} %constant_dynamic-slice_fusion), channel_id=1, source_target_pairs={{0,128},{1,17},{2,130},{3,19},{4,132},{5,21},{6,134},{7,23},{8,136... | collective-permute-start | bytes 393224 | tf_op jit(solution)/shard_map/ppermute | solution.py:191
  10.0 8.8 %collective-permute-start.2 = (bf16[64,1024]{1,0:T(8,128)(2,1)S(1)}, bf16[64,1024]{1,0:T(8,128)(2,1)S(1)}, u32[]{:S(2)}, u32[]{:S(2)}) collective-permute-start(bf16[64,1024]{1,0:T(8,128)(2,1)S(1)} %constant_dynamic-slice_fusion), channel_id=1, source_target_pairs={{0,160},{1,49},{2,162},{3,51},{4,164},{5,53},{6,166},{7,55},{8,168... | collective-permute-start | bytes 393224 | tf_op jit(solution)/shard_map/ppermute | solution.py:191
  12.4 0.7 copy-start.1
  13.0 0.7 copy-start.3
  18.9 11.7 %collective-permute-start.5 = (bf16[256,1024]{1,0:T(8,128)(2,1)S(1)}, bf16[256,1024]{1,0:T(8,128)(2,1)S(1)}, u32[]{:S(2)}, u32[]{:S(2)}) collective-permute-start(bf16[256,1024]{1,0:T(8,128)(2,1)S(1)} %pad_maximum_fusion), channel_id=1, source_target_pairs={{0,64},{1,9},{2,66},{3,11},{4,68},{5,13},{6,70},{7,15},{8,72},{9,1... | collective-permute-start | bytes 1572872 | tf_op jit(solution)/shard_map/ppermute | solution.py:191
  20.4 14.7 %collective-permute-start.3 = (bf16[2064,128]{1,0:T(8,128)(2,1)S(1)}, bf16[2064,128]{1,0:T(8,128)(2,1)S(1)}, u32[]{:S(2)}, u32[]{:S(2)}) collective-permute-start(bf16[2064,128]{1,0:T(8,128)(2,1)S(1)} %get-tuple-element.13.own_ref), channel_id=1, source_target_pairs={{0,1},{1,2},{2,3},{3,4},{4,5},{5,6},{6,7},{8,9},{9,10},{10,11},{11... | collective-permute-start | bytes 1585160 | tf_op jit(solution)/shard_map/ppermute | solution.py:257
  30.6 15.9 %collective-permute-start.7 = (bf16[512,1024]{1,0:T(8,128)(2,1)S(1)}, bf16[512,1024]{1,0:T(8,128)(2,1)S(1)}, u32[]{:S(2)}, u32[]{:S(2)}) collective-permute-start(bf16[512,1024]{1,0:T(8,128)(2,1)S(1)} %constant_dynamic-update-slice_fusion.refs_0_), channel_id=1, source_target_pairs={{0,8},{1,65},{2,10},{3,67},{4,12},{5,69},{6,14},{7,71},{8,16},{9,7... | collective-permute-start | bytes 3145736 | tf_op jit(solution)/shard_map/ppermute | solution.py:191
  31.7 14.9 %collective-permute-start.9 = (bf16[512,1024]{1,0:T(8,128)(2,1)S(1)}, bf16[512,1024]{1,0:T(8,128)(2,1)S(1)}, u32[]{:S(2)}, u32[]{:S(2)}) collective-permute-start(bf16[512,1024]{1,0:T(8,128)(2,1)S(1)} %constant_dynamic-update-slice_fusion.refs_0_), channel_id=1, source_target_pairs={{0,56},{1,193},{2,58},{3,195},{4,60},{5,197},{6,62},{7,199},{8,0},... | collective-permute-start | bytes 3145736 | tf_op jit(solution)/shard_map/ppermute | solution.py:191
  35.9 20.0 %collective-permute-start.4 = (bf16[2064,128]{1,0:T(8,128)(2,1)S(1)}, bf16[2064,128]{1,0:T(8,128)(2,1)S(1)}, u32[]{:S(2)}, u32[]{:S(2)}) collective-permute-start(bf16[2064,128]{1,0:T(8,128)(2,1)S(1)} %shard_map.83), channel_id=1, source_target_pairs={{0,2},{1,3},{2,4},{3,5},{4,6},{5,7},{8,10},{9,11},{10,12},{11,13},... | collective-permute-start | bytes 1585160 | tf_op jit(solution)/shard_map/ppermute | solution.py:270
  39.1 40.4 %collective-permute-start.6 = (bf16[512,1024]{1,0:T(8,128)(2,1)S(1)}, bf16[512,1024]{1,0:T(8,128)(2,1)S(1)}, u32[]{:S(2)}, u32[]{:S(2)}) collective-permute-start(bf16[512,1024]{1,0:T(8,128)(2,1)S(1)} %constant_dynamic-update-slice_fusion.refs_0_), channel_id=1, source_target_pairs={{0,1},{1,0},{2,3},{3,2},{4,5},{5,4},{6,7},{7,6},{8,9},{9,8},{10,11... | collective-permute-start | bytes 3145736 | tf_op jit(solution)/shard_map/ppermute | solution.py:195
  46.5 9.4 %collective-permute-start.11 = (bf16[256,1024]{1,0:T(8,128)(2,1)S(1)}, bf16[256,1024]{1,0:T(8,128)(2,1)S(1)}, u32[]{:S(2)}, u32[]{:S(2)}) collective-permute-start(bf16[256,1024]{1,0:T(8,128)(2,1)S(1)} %slice.8), channel_id=1, source_target_pairs={{0,8},{1,65},{2,10},{3,67},{4,12},{5,69},{6,14},{7,71},{8,16},{9,7... | collective-permute-start | bytes 1572872 | tf_op jit(solution)/shard_map/ppermute | solution.py:191
  46.7 16.3 %collective-permute-start.13 = (bf16[256,1024]{1,0:T(8,128)(2,1)S(1)}, bf16[256,1024]{1,0:T(8,128)(2,1)S(1)}, u32[]{:S(2)}, u32[]{:S(2)}) collective-permute-start(bf16[256,1024]{1,0:T(8,128)(2,1)S(1)} %slice.9), channel_id=1, source_target_pairs={{0,56},{1,193},{2,58},{3,195},{4,60},{5,197},{6,62},{7,199},{8,0},... | collective-permute-start | bytes 1572872 | tf_op jit(solution)/shard_map/ppermute | solution.py:191
  49.4 30.1 %collective-permute-start.10 = (bf16[512,1024]{1,0:T(8,128)(2,1)S(1)}, bf16[512,1024]{1,0:T(8,128)(2,1)S(1)}, u32[]{:S(2)}, u32[]{:S(2)}) collective-permute-start(bf16[512,1024]{1,0:T(8,128)(2,1)S(1)} %collective-permute-done.9.refs_2_), channel_id=1, source_target_pairs={{0,1},{1,0},{2,3},{3,2},{4,5},{5,4},{6,7},{7,6},{8,9},{9,8},{10,11... | collective-permute-start | bytes 3145736 | tf_op jit(solution)/shard_map/ppermute | solution.py:195
  55.9 23.6 %collective-permute-start.8 = (bf16[512,1024]{1,0:T(8,128)(2,1)S(1)}, bf16[512,1024]{1,0:T(8,128)(2,1)S(1)}, u32[]{:S(2)}, u32[]{:S(2)}) collective-permute-start(bf16[512,1024]{1,0:T(8,128)(2,1)S(1)} %collective-permute-done.7.refs_1_), channel_id=1, source_target_pairs={{0,1},{1,0},{2,3},{3,2},{4,5},{5,4},{6,7},{7,6},{8,9},{9,8},{10,11... | collective-permute-start | bytes 3145736 | tf_op jit(solution)/shard_map/ppermute | solution.py:195
  55.9 23.6 %collective-permute-start.12 = (bf16[256,1024]{1,0:T(8,128)(2,1)S(1)}, bf16[256,1024]{1,0:T(8,128)(2,1)S(1)}, u32[]{:S(2)}, u32[]{:S(2)}) collective-permute-start(bf16[256,1024]{1,0:T(8,128)(2,1)S(1)} %collective-permute-done.11.refs_3_), channel_id=1, source_target_pairs={{0,1},{1,0},{2,3},{3,2},{4,5},{5,4},{6,7},{7,6},{8,9},{9,8},{10,11... | collective-permute-start | bytes 1572872 | tf_op jit(solution)/shard_map/ppermute | solution.py:195
  62.9 16.5 %collective-permute-start.14 = (bf16[256,1024]{1,0:T(8,128)(2,1)S(1)}, bf16[256,1024]{1,0:T(8,128)(2,1)S(1)}, u32[]{:S(2)}, u32[]{:S(2)}) collective-permute-start(bf16[256,1024]{1,0:T(8,128)(2,1)S(1)} %collective-permute-done.13.refs_4_), channel_id=1, source_target_pairs={{0,1},{1,0},{2,3},{3,2},{4,5},{5,4},{6,7},{7,6},{8,9},{9,8},{10,11... | collective-permute-start | bytes 1572872 | tf_op jit(solution)/shard_map/ppermute | solution.py:195
  62.9 6.6 %copy-start.2 = (f32[2048]{0:T(1024)S(1)}, f32[2048]{0:T(1024)}, u32[]{:S(2)}) copy-start(f32[2048]{0:T(1024)} %param.14) | copy-start | bytes 24580

commit v2 on v1

--- a/solution.py
+++ b/solution.py
@@ -145,7 +145,7 @@
 
 
 def project_kernel(owner, g_ref, *refs):
-    pieces, (out_ref, w_ref) = refs[:5], refs[-2:]
+    pieces, (out_ref, w_ref) = refs[:PIECES], refs[-2:]
     pack = lax.axis_index("pack")
     core = lax.axis_index("hist") % 2
     oc = core if owner == 0 else 1 - core
@@ -164,16 +164,18 @@
 
 
 SMALL = [
-    [(0, 0), (0, -4), (-2, 0), (-2, -4), (-1, 0), (-1, -4), (-3, 0), (-3, -4)],
-    [(0, 0), (0, -4), (0, -2), (0, 2), (0, -1), (0, -5), (0, -3), (0, 1)],
+    [(0, 0), (-1, 0), (0, -4), (-1, -4), (-2, 0), (-3, 0), (-2, -4), (1, -4)],
+    [(0, 0), (0, -1), (0, 1), (0, 2), (0, -2), (0, -3), (0, 3), (0, -4)],
 ]
 
 
 def turned(d):
-    return [((y0, z0 + d), (y1 + d, z1)) for (y0, z0), (y1, z1) in zip(*SMALL)]
-
-
-SHARDS = [turned(0), turned(-1), turned(1), turned(-2)[:4], turned(2)[4:]]
+    both = [((y0, z0 + d), (y1 + d, z1)) for (y0, z0), (y1, z1) in zip(*SMALL)]
+    return both[:4], both[4:]
+
+
+SHARDS = [*turned(0), *turned(-1), *turned(1), turned(-2)[0], turned(2)[1]]
+PIECES = len(SHARDS)
 
 
 def moves(*ways):
@@ -195,24 +197,25 @@
     return lax.ppermute(x, BOTH, [(i, i ^ 1) for i in range(NY * NZ * NH)])
 
 
-def gather_first(w):
+def gather(w):
     core = lax.axis_index("hist") % 2
     x = lax.dynamic_slice_in_dim(w, core * 1024, 1024, 1)
-    return x, send(x, (0, 4), (0, 4)), send(x, (2, 0), (0, 2)), send(x, (2, 4), (0, -2))
-
-
-def gather_second(parts):
-    x = jnp.concatenate(parts, 0)
-    return x, send(x, (1, 0), (0, 1))
-
-
-def gather_third(parts):
-    x = jnp.concatenate(parts, 0)
-    return x, send(x, (0, 1), (1, 0)), send(x, (0, -1), (-1, 0))
-
-
-def gather_fourth(x, a, b):
-    return x, a, b, send(a[:256], (0, 1), (1, 0)), send(b[256:], (0, -1), (-1, 0))
+    a1 = send(x, (1, 0), (0, 1))
+    a2 = send(x, (0, 4), (0, -1))
+    b1 = send(a1, (1, 0), (0, 1))
+    b2 = send(a2, (1, 0), (0, -1))
+    c1 = send(b1, (1, 0), (0, 1))
+    c2 = send(b2, (1, 0), (0, -1))
+    d1 = send(jnp.where(core == 0, a2, c1), (-1, 0), (0, 1))
+    one = jnp.concatenate([x, a1, a2, b2], 0)
+    two = jnp.concatenate([b1, c1, c2, d1], 0)
+    up1 = send(one, (0, 1), (1, 0))
+    down1 = send(one, (0, -1), (-1, 0))
+    up2 = send(two, (0, 1), (1, 0))
+    down2 = send(two, (0, -1), (-1, 0))
+    far1 = send(up1, (0, 1), (1, 0))
+    far2 = send(down2, (0, -1), (-1, 0))
+    return one, two, up1, up2, down1, down2, far1, far2
 
 
 def call(kernel, grid, in_specs, out_specs, out_shape, scratch, flops, nbytes, vmem=14, alias=None):
@@ -245,15 +248,13 @@
     pay_shape = shape((PAYLOAD, HEAD), BF16)
     mb = 1 << 20
 
-    first = gather_first(w_out)
-
+    pieces = gather(w_out)
+    others = [swapped(p) for p in pieces]
     own, mid = call(
         state_kernel, (steps,), [smem, users, block, block], (full, heads),
         (pay_shape, shape((HEADS, HEAD, HEAD), BF16)),
         [pltpu.VMEM((2, HALF, HEAD), F32)], 270 * 10**6, 5 * mb,
     )(forget_rate, user_ids, k, v)
-    first, own = lax.optimization_barrier((first, own))
-    second = gather_second(first)
     one = lax.ppermute(own, "hist", [(i, i + 1) for i in range(NH - 1)])
     part = call(
         inner_kernel, (steps,), [smem, users, block, block, block, heads], block,
@@ -261,9 +262,6 @@
         [pltpu.VMEM((HALF, HALF), F32), pltpu.VMEM((2, HALF, HALF), F32), pltpu.VMEM((HALF, HEAD), F32)],
         1200 * 10**6, 11 * mb,
     )(forget_rate, user_ids, q, k, v, mid)
-    third = gather_third(second)
-    pieces = gather_fourth(*third)
-    others = [swapped(p) for p in pieces]
     pair = call(
         pair_kernel, (1,), [smem, users, full, full], full, pay_shape, [], 10**6, 3 * mb // 2
     )(forget_rate, user_ids, own, one)
@@ -284,10 +282,10 @@
 
         mixed = call(
             functools.partial(project_kernel, owner), (2,),
-            [pl.BlockSpec(memory_space=pltpu.VMEM)] * 6 + [pl.BlockSpec(memory_space=pl.ANY)] * owner,
+            [pl.BlockSpec(memory_space=pltpu.VMEM)] * (1 + PIECES) + [pl.BlockSpec(memory_space=pl.ANY)] * owner,
             pl.BlockSpec((ROWS, 512), column), shape((ROWS, WIDTH), BF16),
             [pltpu.VMEM((WIDTH, 1024), BF16)],
-            2150 * 10**6, 7 * mb, 14, {6: 0} if owner else None,
+            2150 * 10**6, 7 * mb, 14, {1 + PIECES: 0} if owner else None,
         )(gated, *got, *([mixed] if owner else []))
     return mixed[None]
 

time: 84.3 us -> 77.9 us (0.924)
  starting transfers between devices: 48.6 us -> 31.7 us
  waiting for transfers between devices: 6.82 us -> 17.8 us
    ppermute x5 -> x8, starting transfers between devices: 18.5 us -> 5.42 us  [swapped(): return lax.ppermute(x, BOTH, [(i, i ^ 1) for i in range(NY * NZ * NH)])]
    ppermute x8 -> x13, waiting for transfers between devices: 5.08 us -> 13.3 us  [send(): return lax.ppermute(x, BOTH, moves(*ways))]
    ppermute x1, waiting for transfers between devices: 0.01 us -> 4.43 us  [local(): two = lax.ppermute(pair, 'hist', [(i, i + 2) for i in range(NH - 2)])]
    ppermute x1, starting transfers between devices: 8.5 us -> 4.79 us  [local(): one = lax.ppermute(own, 'hist', [(i, i + 1) for i in range(NH - 1)])]
    ppermute x1, waiting for transfers between devices: 1.73 us -> 0.01 us  [local(): one = lax.ppermute(own, 'hist', [(i, i + 1) for i in range(NH - 1)])]
    ppermute x8 -> x13, starting transfers between devices: 18.5 us -> 18.3 us  [send(): return lax.ppermute(x, BOTH, moves(*ways))]
    unnamed x12 -> x14, local copies, waits for them, and re-layouts: 2.33 us -> 2.32 us
  transfers between devices with their start and end apart: 15 -> 23, of which waited for: 4 -> 8; matrix products, arithmetic and copies ran while one was open for 0% -> 0% of each run, Pallas kernels for 26% -> 28%
where the time goes in v2:
time: 77.9 us; the launch traced here: 77.5 us
  starting transfers between devices  31.7 us (41%)
  Pallas kernels  25.4 us (33%)
  waiting for transfers between devices  17.8 us (23%)
  local copies, waits for them, and re-layouts  2.34 us (3%)
    ppermute x13, starting transfers between devices, send(): return lax.ppermute(x, BOTH, moves(*ways))  18.3 us
    ppermute x13, waiting for transfers between devices, send(): return lax.ppermute(x, BOTH, moves(*ways))  13.3 us
    pallas_call x2, Pallas kernels, local(): call(functools.partial(project_kernel, owner), (2,), [pl.BlockSpec(memory...  7.79 us
    pallas_call x1, Pallas kernels, local(): call(inner_kernel, (steps,), [smem, users, block, block, block, heads], b...  6.58 us
    pallas_call x1, Pallas kernels, local(): call(gate_kernel, (steps,), [smem, users, full, full, block, block, block...  6.15 us
    ppermute x8, starting transfers between devices, swapped(): return lax.ppermute(x, BOTH, [(i, i ^ 1) for i in range(NY * NZ * NH)])  5.42 us
    ppermute x1, starting transfers between devices, local(): one = lax.ppermute(own, 'hist', [(i, i + 1) for i in range(NH - 1)])  4.79 us
    ppermute x1, waiting for transfers between devices, local(): two = lax.ppermute(pair, 'hist', [(i, i + 2) for i in range(NH - 2)])  4.43 us
  transfers between devices with their start and end apart: 23, of which 8 were waited for; matrix products, arithmetic and copies ran while one was open for 0% of the time, Pallas kernels for 28%

profile of v2, /device:TPU:1, one launch (start us, length us, event | category | flops | bytes accessed | tf_op | source)
XLA Modules:
  0.0 77.5 jit_solution(15086366686008353487)
XLA Ops:
  0.0 0.0 copy-start
  0.0 0.9 %copy-done = bf16[64,2048]{1,0:T(8,128)(2,1)S(1)} copy-done((bf16[64,2048]{1,0:T(8,128)(2,1)S(1)}, bf16[64,2048]{1,0:T(8,128)(2,1)}, u32[]{:S(2)}) %copy-start) | copy-done | bytes 262168
  1.0 2.5 %collective-permute-start.2 = (bf16[64,1024]{1,0:T(8,128)(2,1)S(1)}, bf16[64,1024]{1,0:T(8,128)(2,1)S(1)}, u32[]{:S(2)}, u32[]{:S(2)}) collective-permute-start(bf16[64,1024]{1,0:T(8,128)(2,1)S(1)} %constant_dynamic-slice_fusion), channel_id=1, source_target_pairs={{0,64},{1,9},{2,66},{3,11},{4,68},{5,13},{6,70},{7,15},{8,72},{9,1... | collective-permute-start | bytes 393224 | tf_op jit(solution)/shard_map/ppermute | solution.py:193
  3.5 4.0 %collective-permute-start.3 = (bf16[64,1024]{1,0:T(8,128)(2,1)S(1)}, bf16[64,1024]{1,0:T(8,128)(2,1)S(1)}, u32[]{:S(2)}, u32[]{:S(2)}) collective-permute-start(bf16[64,1024]{1,0:T(8,128)(2,1)S(1)} %constant_dynamic-slice_fusion), channel_id=1, source_target_pairs={{0,32},{1,57},{2,34},{3,59},{4,36},{5,61},{6,38},{7,63},{8,40},{9,... | collective-permute-start | bytes 393224 | tf_op jit(solution)/shard_map/ppermute | solution.py:193
  7.5 2.5 %collective-permute-done.2 = bf16[64,1024]{1,0:T(8,128)(2,1)S(1)} collective-permute-done((bf16[64,1024]{1,0:T(8,128)(2,1)S(1)}, bf16[64,1024]{1,0:T(8,128)(2,1)S(1)}, u32[]{:S(2)}, u32[]{:S(2)}) %collective-permute-start.2) | collective-permute-done | bytes 131104 | tf_op jit(solution)/shard_map/ppermute | solution.py:193
  10.0 0.0 collective-permute-start.6
  10.0 0.0 collective-permute-done.3
  10.0 2.8 %collective-permute-start.4 = (bf16[64,1024]{1,0:T(8,128)(2,1)S(1)}, bf16[64,1024]{1,0:T(8,128)(2,1)S(1)}, u32[]{:S(2)}, u32[]{:S(2)}) collective-permute-start(bf16[64,1024]{1,0:T(8,128)(2,1)S(1)} %collective-permute-done.3), channel_id=1, source_target_pairs={{0,64},{1,57},{2,66},{3,59},{4,68},{5,61},{6,70},{7,63},{8,72},{9,... | collective-permute-start | bytes 393224 | tf_op jit(solution)/shard_map/ppermute | solution.py:193
  12.8 3.5 %collective-permute-done.6 = bf16[64,1024]{1,0:T(8,128)(2,1)S(1)} collective-permute-done((bf16[64,1024]{1,0:T(8,128)(2,1)S(1)}, bf16[64,1024]{1,0:T(8,128)(2,1)S(1)}, u32[]{:S(2)}, u32[]{:S(2)}) %collective-permute-start.6) | collective-permute-done | bytes 131104 | tf_op jit(solution)/shard_map/ppermute | solution.py:193
  16.3 0.0 collective-permute-start.7
  16.3 0.0 copy-start.1
  16.3 0.7 copy-done.1
  17.0 0.0 copy-start.4
  17.0 0.7 copy-done.4
  17.7 4.0 %shard_map.82 = (bf16[2064,128]{1,0:T(8,128)(2,1)S(1)}, bf16[16,128,128]{2,1,0:T(8,128)(2,1)S(1)}) custom-call(f32[16]{0:T(128)S(1)} %copy-done.4, s32[1,512]{1,0:T(1,128)S(1)} %copy-done.1, bf16[512,2048]{1,0:T(8,128)(2,1)} %bitcast.9, bf16[512,2048]{1,0:T(8,128)(2,1)} %bitcast.11), custom_call_target="tpu_custom_call" | custom-call | flops 270000000 | bytes 5242880 | tf_op jit(solution)/shard_map/pallas_call | solution.py:253
  21.7 0.0 copy-start.2
  21.7 0.0 copy-start.5
  21.7 4.8 %collective-permute-start = (bf16[2064,128]{1,0:T(8,128)(2,1)S(1)}, bf16[2064,128]{1,0:T(8,128)(2,1)S(1)}, u32[]{:S(2)}, u32[]{:S(2)}) collective-permute-start(bf16[2064,128]{1,0:T(8,128)(2,1)S(1)} %get-tuple-element.7.own_ref), channel_id=1, source_target_pairs={{0,1},{1,2},{2,3},{3,4},{4,5},{5,6},{6,7},{8,9},{9,10},{10,11},{11... | collective-permute-start | bytes 1585160 | tf_op jit(solution)/shard_map/ppermute | solution.py:258
  26.5 0.0 collective-permute-done.4
  26.5 4.3 %collective-permute-start.8 = (bf16[64,1024]{1,0:T(8,128)(2,1)S(1)}, bf16[64,1024]{1,0:T(8,128)(2,1)S(1)}, u32[]{:S(2)}, u32[]{:S(2)}) collective-permute-start(bf16[64,1024]{1,0:T(8,128)(2,1)S(1)} %collective-permute-done.4), channel_id=1, source_target_pairs={{0,64},{1,57},{2,66},{3,59},{4,68},{5,61},{6,70},{7,63},{8,72},{9,... | collective-permute-start | bytes 393224 | tf_op jit(solution)/shard_map/ppermute | solution.py:193
  30.8 0.0 collective-permute-done.7
  30.8 0.1 collective-permute-start.9
  31.0 0.1 collective-permute-start.11
  31.1 2.7 %collective-permute-start.15 = (bf16[256,1024]{1,0:T(8,128)(2,1)S(1)}, bf16[256,1024]{1,0:T(8,128)(2,1)S(1)}, u32[]{:S(2)}, u32[]{:S(2)}) collective-permute-start(bf16[256,1024]{1,0:T(8,128)(2,1)S(1)} %pad_maximum_fusion.refs_0_), channel_id=1, source_target_pairs={{0,56},{1,193},{2,58},{3,195},{4,60},{5,197},{6,62},{7,199},{8,0},... | collective-permute-start | bytes 1572872 | tf_op jit(solution)/shard_map/ppermute | solution.py:193
  33.7 0.0 collective-permute-done.8
  33.7 0.0 collective-permute-start.5
  33.8 3.9 %collective-permute-done.9 = bf16[64,1024]{1,0:T(8,128)(2,1)S(1)} collective-permute-done((bf16[64,1024]{1,0:T(8,128)(2,1)S(1)}, bf16[64,1024]{1,0:T(8,128)(2,1)S(1)}, u32[]{:S(2)}, u32[]{:S(2)}) %collective-permute-start.9) | collective-permute-done | bytes 131104 | tf_op jit(solution)/shard_map/ppermute | solution.py:193
  37.7 1.6 %collective-permute-start.17 = (bf16[256,1024]{1,0:T(8,128)(2,1)S(1)}, bf16[256,1024]{1,0:T(8,128)(2,1)S(1)}, u32[]{:S(2)}, u32[]{:S(2)}) collective-permute-start(bf16[256,1024]{1,0:T(8,128)(2,1)S(1)} %constant_dynamic-update-slice_fusion.refs_1_), channel_id=1, source_target_pairs={{0,56},{1,193},{2,58},{3,195},{4,60},{5,197},{6,62},{7,199},{8,0},... | collective-permute-start | bytes 1572872 | tf_op jit(solution)/shard_map/ppermute | solution.py:193
  39.2 0.0 collective-permute-done.one_ref
  39.2 0.0 collective-permute-start.13
  39.2 0.0 copy-done.2
  39.2 0.0 copy-done.5
  39.3 0.9 %shard_map.83 = bf16[2064,128]{1,0:T(8,128)(2,1)S(1)} custom-call(f32[16]{0:T(128)S(1)} %copy-done.5, s32[1,512]{1,0:T(1,128)S(1)} %copy-done.2, bf16[2064,128]{1,0:T(8,128)(2,1)S(1)} %get-tuple-element.7.own_ref, bf16[2064,128]{1,0:T(8,128)(2,1)S(1)} %collective-permute-done.one_ref), custom_call_target="tpu_custom_call" | custom-call | flops 1000000 | bytes 1572864 | tf_op jit(solution)/shard_map/pallas_call | solution.py:265
  40.1 0.5 collective-permute-done.11.refs_2_
  40.6 3.1 %collective-permute-start.1 = (bf16[2064,128]{1,0:T(8,128)(2,1)S(1)}, bf16[2064,128]{1,0:T(8,128)(2,1)S(1)}, u32[]{:S(2)}, u32[]{:S(2)}) collective-permute-start(bf16[2064,128]{1,0:T(8,128)(2,1)S(1)} %shard_map.83), channel_id=1, source_target_pairs={{0,2},{1,3},{2,4},{3,5},{4,6},{5,7},{8,10},{9,11},{10,12},{11,13},... | collective-permute-start | bytes 1585160 | tf_op jit(solution)/shard_map/ppermute | solution.py:268
  43.7 0.0 collective-permute-done.15.refs_4_
  43.8 1.8 %collective-permute-start.10 = (bf16[256,1024]{1,0:T(8,128)(2,1)S(1)}, bf16[256,1024]{1,0:T(8,128)(2,1)S(1)}, u32[]{:S(2)}, u32[]{:S(2)}) collective-permute-start(bf16[256,1024]{1,0:T(8,128)(2,1)S(1)} %constant_dynamic-update-slice_fusion.refs_1_), channel_id=1, source_target_pairs={{0,1},{1,0},{2,3},{3,2},{4,5},{5,4},{6,7},{7,6},{8,9},{9,8},{10,11... | collective-permute-start | bytes 1572872 | tf_op jit(solution)/shard_map/ppermute | solution.py:197
  45.6 0.0 collective-permute-done.5.refs_0_
  45.6 0.0 collective-permute-start.19
  45.6 0.5 collective-permute-done.17.refs_5_
  46.1 0.0 collective-permute-start.12
  46.1 2.4 %collective-permute-done.13.refs_3_ = bf16[256,1024]{1,0:T(8,128)(2,1)S(1)} collective-permute-done((bf16[256,1024]{1,0:T(8,128)(2,1)S(1)}, bf16[256,1024]{1,0:T(8,128)(2,1)S(1)}, u32[]{:S(2)}, u32[]{:S(2)}) %collective-permute-start.13) | collective-permute-done | bytes 524320 | tf_op jit(solution)/shard_map/ppermute | solution.py:193
  48.5 0.3 collective-permute-start.21
  48.8 0.0 collective-permute-done.10.refs_1_
  48.8 0.4 collective-permute-start.16
  49.2 4.4 %collective-permute-done.1.two_ref = bf16[2064,128]{1,0:T(8,128)(2,1)S(1)} collective-permute-done((bf16[2064,128]{1,0:T(8,128)(2,1)S(1)}, bf16[2064,128]{1,0:T(8,128)(2,1)S(1)}, u32[]{:S(2)}, u32[]{:S(2)}) %collective-permute-start.1) | collective-permute-done | bytes 528416 | tf_op jit(solution)/shard_map/ppermute | solution.py:268
  53.6 2.3 %collective-permute-start.18 = (bf16[256,1024]{1,0:T(8,128)(2,1)S(1)}, bf16[256,1024]{1,0:T(8,128)(2,1)S(1)}, u32[]{:S(2)}, u32[]{:S(2)}) collective-permute-start(bf16[256,1024]{1,0:T(8,128)(2,1)S(1)} %collective-permute-done.17.refs_5_), channel_id=1, source_target_pairs={{0,1},{1,0},{2,3},{3,2},{4,5},{5,4},{6,7},{7,6},{8,9},{9,8},{10,11... | collective-permute-start | bytes 1572872 | tf_op jit(solution)/shard_map/ppermute | solution.py:197
  55.9 0.0 collective-permute-done.19.refs_6_
  55.9 0.1 collective-permute-start.14
  56.1 0.0 collective-permute-done.12.refs_2_
  56.1 0.4 collective-permute-start.20
  56.4 0.1 collective-permute-done.21.refs_7_
  56.5 0.4 collective-permute-start.22
  56.9 0.0 copy-start.3
  56.9 6.6 %shard_map.84.part_ref = f32[512,2048]{1,0:T(8,128)S(1)} custom-call(f32[16]{0:T(128)S(1)} %copy-done.5, s32[1,512]{1,0:T(1,128)S(1)} %copy-done.2, bf16[512,2048]{1,0:T(8,128)(2,1)} %bitcast.7, bf16[512,2048]{1,0:T(8,128)(2,1)} %bitcast.10, bf16[512,2048]{1,0:T(8,128)(2,1)} %bitcast.12, bf16[16,128,128]{2,1,0:T(8,128)(2,1)S(1)} %get-tuple-element.8.mid_ref), custom_call_target="tpu_custom_call" | custom-call | flops 1200000000 | bytes 11534336 | tf_op jit(solution)/shard_map/pallas_call | solution.py:259
  63.5 0.0 copy-done.3
  63.5 6.1 %shard_map.85.g_ref = bf16[512,2048]{1,0:T(8,128)(2,1)S(1)} custom-call(f32[16]{0:T(128)S(1)} %copy-done.5, s32[1,512]{1,0:T(1,128)S(1)} %copy-done.2, bf16[2064,128]{1,0:T(8,128)(2,1)S(1)} %collective-permute-done.one_ref, bf16[2064,128]{1,0:T(8,128)(2,1)S(1)} %collective-permute-done.1.two_ref, bf16[512,2048]{1,0:T(8,128)(2,1)} %bitcast.8, ...), custom_call_target="tpu_custom_call" | custom-call | flops 300000000 | bytes 11534336 | tf_op jit(solution)/shard_map/pallas_call | solution.py:269
  69.6 3.9 %shard_map.86.refs_8_ = bf16[512,2048]{1,0:T(8,128)(2,1)} custom-call(bf16[512,2048]{1,0:T(8,128)(2,1)S(1)} %shard_map.85.g_ref, bf16[256,1024]{1,0:T(8,128)(2,1)S(1)} %pad_maximum_fusion.refs_0_, bf16[256,1024]{1,0:T(8,128)(2,1)S(1)} %constant_dynamic-update-slice_fusion.refs_1_, bf16[256,1024]{1,0:T(8,128)(2,1)S(1)} %collective-permute-done.11.refs_2_, ...), custom_call_target="tpu_custom_call" | custom-call | flops 2150000128 | bytes 7340032 | tf_op jit(solution)/shard_map/pallas_call | solution.py:283
  73.5 0.0 collective-permute-done.16.refs_4_
  73.5 0.0 collective-permute-done.14.refs_3_
  73.5 0.0 collective-permute-done.18.refs_5_
  73.5 0.0 collective-permute-done.20.refs_6_
  73.5 0.0 collective-permute-done.22.refs_7_
  73.6 3.9 %shard_map.87 = bf16[512,2048]{1,0:T(8,128)(2,1)} custom-call(bf16[512,2048]{1,0:T(8,128)(2,1)S(1)} %shard_map.85.g_ref, bf16[256,1024]{1,0:T(8,128)(2,1)S(1)} %collective-permute-done.5.refs_0_, bf16[256,1024]{1,0:T(8,128)(2,1)S(1)} %collective-permute-done.10.refs_1_, ...), custom_call_target="tpu_custom_call", output_to_operand_aliasing={{}: (9, {})} | custom-call | flops 2150000128 | bytes 7340032 | tf_op jit(solution)/shard_map/pallas_call | solution.py:283
  (6 shorter events, 0.1 us)
Async XLA Ops:
  0.0 1.0 %copy-start = (bf16[64,2048]{1,0:T(8,128)(2,1)S(1)}, bf16[64,2048]{1,0:T(8,128)(2,1)}, u32[]{:S(2)}) copy-start(bf16[64,2048]{1,0:T(8,128)(2,1)} %param.15) | copy-start | bytes 786436
  1.0 9.1 %collective-permute-start.2 = (bf16[64,1024]{1,0:T(8,128)(2,1)S(1)}, bf16[64,1024]{1,0:T(8,128)(2,1)S(1)}, u32[]{:S(2)}, u32[]{:S(2)}) collective-permute-start(bf16[64,1024]{1,0:T(8,128)(2,1)S(1)} %constant_dynamic-slice_fusion), channel_id=1, source_target_pairs={{0,64},{1,9},{2,66},{3,11},{4,68},{5,13},{6,70},{7,15},{8,72},{9,1... | collective-permute-start | bytes 393224 | tf_op jit(solution)/shard_map/ppermute | solution.py:193
  3.5 6.5 %collective-permute-start.3 = (bf16[64,1024]{1,0:T(8,128)(2,1)S(1)}, bf16[64,1024]{1,0:T(8,128)(2,1)S(1)}, u32[]{:S(2)}, u32[]{:S(2)}) collective-permute-start(bf16[64,1024]{1,0:T(8,128)(2,1)S(1)} %constant_dynamic-slice_fusion), channel_id=1, source_target_pairs={{0,32},{1,57},{2,34},{3,59},{4,36},{5,61},{6,38},{7,63},{8,40},{9,... | collective-permute-start | bytes 393224 | tf_op jit(solution)/shard_map/ppermute | solution.py:193
  10.0 6.3 %collective-permute-start.6 = (bf16[64,1024]{1,0:T(8,128)(2,1)S(1)}, bf16[64,1024]{1,0:T(8,128)(2,1)S(1)}, u32[]{:S(2)}, u32[]{:S(2)}) collective-permute-start(bf16[64,1024]{1,0:T(8,128)(2,1)S(1)} %collective-permute-done.2), channel_id=1, source_target_pairs={{0,64},{1,9},{2,66},{3,11},{4,68},{5,13},{6,70},{7,15},{8,72},{9,1... | collective-permute-start | bytes 393224 | tf_op jit(solution)/shard_map/ppermute | solution.py:193
  10.0 16.5 %collective-permute-start.4 = (bf16[64,1024]{1,0:T(8,128)(2,1)S(1)}, bf16[64,1024]{1,0:T(8,128)(2,1)S(1)}, u32[]{:S(2)}, u32[]{:S(2)}) collective-permute-start(bf16[64,1024]{1,0:T(8,128)(2,1)S(1)} %collective-permute-done.3), channel_id=1, source_target_pairs={{0,64},{1,57},{2,66},{3,59},{4,68},{5,61},{6,70},{7,63},{8,72},{9,... | collective-permute-start | bytes 393224 | tf_op jit(solution)/shard_map/ppermute | solution.py:193
  16.3 14.5 %collective-permute-start.7 = (bf16[64,1024]{1,0:T(8,128)(2,1)S(1)}, bf16[64,1024]{1,0:T(8,128)(2,1)S(1)}, u32[]{:S(2)}, u32[]{:S(2)}) collective-permute-start(bf16[64,1024]{1,0:T(8,128)(2,1)S(1)} %collective-permute-done.6), channel_id=1, source_target_pairs={{0,64},{1,9},{2,66},{3,11},{4,68},{5,13},{6,70},{7,15},{8,72},{9,1... | collective-permute-start | bytes 393224 | tf_op jit(solution)/shard_map/ppermute | solution.py:193
  16.3 0.7 copy-start.1
  17.0 0.7 copy-start.4
  21.7 17.6 %copy-start.2 = (s32[1,512]{1,0:T(1,128)S(1)}, s32[1,512]{1,0:T(1,128)}, u32[]{:S(2)}) copy-start(s32[1,512]{1,0:T(1,128)} %u_ref.7) | copy-start | bytes 6148
  21.7 17.6 %copy-start.5 = (f32[16]{0:T(128)S(1)}, f32[16]{0:T(128)}, u32[]{:S(2)}) copy-start(f32[16]{0:T(128)} %rate_ref.7) | copy-start | bytes 196
  21.7 17.5 %collective-permute-start = (bf16[2064,128]{1,0:T(8,128)(2,1)S(1)}, bf16[2064,128]{1,0:T(8,128)(2,1)S(1)}, u32[]{:S(2)}, u32[]{:S(2)}) collective-permute-start(bf16[2064,128]{1,0:T(8,128)(2,1)S(1)} %get-tuple-element.7.own_ref), channel_id=1, source_target_pairs={{0,1},{1,2},{2,3},{3,4},{4,5},{5,6},{6,7},{8,9},{9,10},{10,11},{11... | collective-permute-start | bytes 1585160 | tf_op jit(solution)/shard_map/ppermute | solution.py:258
  26.5 7.2 %collective-permute-start.8 = (bf16[64,1024]{1,0:T(8,128)(2,1)S(1)}, bf16[64,1024]{1,0:T(8,128)(2,1)S(1)}, u32[]{:S(2)}, u32[]{:S(2)}) collective-permute-start(bf16[64,1024]{1,0:T(8,128)(2,1)S(1)} %collective-permute-done.4), channel_id=1, source_target_pairs={{0,64},{1,57},{2,66},{3,59},{4,68},{5,61},{6,70},{7,63},{8,72},{9,... | collective-permute-start | bytes 393224 | tf_op jit(solution)/shard_map/ppermute | solution.py:193
  30.8 6.8 %collective-permute-start.9 = (bf16[64,1024]{1,0:T(8,128)(2,1)S(1)}, bf16[64,1024]{1,0:T(8,128)(2,1)S(1)}, u32[]{:S(2)}, u32[]{:S(2)}) collective-permute-start(bf16[64,1024]{1,0:T(8,128)(2,1)S(1)} %get-tuple-element.9), channel_id=1, source_target_pairs={{0,192},{1,9},{2,194},{3,11},{4,196},{5,13},{6,198},{7,15},{8,200}... | collective-permute-start | bytes 393224 | tf_op jit(solution)/shard_map/ppermute | solution.py:193
  31.0 9.6 %collective-permute-start.11 = (bf16[256,1024]{1,0:T(8,128)(2,1)S(1)}, bf16[256,1024]{1,0:T(8,128)(2,1)S(1)}, u32[]{:S(2)}, u32[]{:S(2)}) collective-permute-start(bf16[256,1024]{1,0:T(8,128)(2,1)S(1)} %pad_maximum_fusion.refs_0_), channel_id=1, source_target_pairs={{0,8},{1,65},{2,10},{3,67},{4,12},{5,69},{6,14},{7,71},{8,16},{9,7... | collective-permute-start | bytes 1572872 | tf_op jit(solution)/shard_map/ppermute | solution.py:193
  31.1 12.7 %collective-permute-start.15 = (bf16[256,1024]{1,0:T(8,128)(2,1)S(1)}, bf16[256,1024]{1,0:T(8,128)(2,1)S(1)}, u32[]{:S(2)}, u32[]{:S(2)}) collective-permute-start(bf16[256,1024]{1,0:T(8,128)(2,1)S(1)} %pad_maximum_fusion.refs_0_), channel_id=1, source_target_pairs={{0,56},{1,193},{2,58},{3,195},{4,60},{5,197},{6,62},{7,199},{8,0},... | collective-permute-start | bytes 1572872 | tf_op jit(solution)/shard_map/ppermute | solution.py:193
  33.7 11.8 %collective-permute-start.5 = (bf16[256,1024]{1,0:T(8,128)(2,1)S(1)}, bf16[256,1024]{1,0:T(8,128)(2,1)S(1)}, u32[]{:S(2)}, u32[]{:S(2)}) collective-permute-start(bf16[256,1024]{1,0:T(8,128)(2,1)S(1)} %pad_maximum_fusion.refs_0_), channel_id=1, source_target_pairs={{0,1},{1,0},{2,3},{3,2},{4,5},{5,4},{6,7},{7,6},{8,9},{9,8},{10,11... | collective-permute-start | bytes 1572872 | tf_op jit(solution)/shard_map/ppermute | solution.py:197
  37.7 8.4 %collective-permute-start.17 = (bf16[256,1024]{1,0:T(8,128)(2,1)S(1)}, bf16[256,1024]{1,0:T(8,128)(2,1)S(1)}, u32[]{:S(2)}, u32[]{:S(2)}) collective-permute-start(bf16[256,1024]{1,0:T(8,128)(2,1)S(1)} %constant_dynamic-update-slice_fusion.refs_1_), channel_id=1, source_target_pairs={{0,56},{1,193},{2,58},{3,195},{4,60},{5,197},{6,62},{7,199},{8,0},... | collective-permute-start | bytes 1572872 | tf_op jit(solution)/shard_map/ppermute | solution.py:193
  39.2 9.2 %collective-permute-start.13 = (bf16[256,1024]{1,0:T(8,128)(2,1)S(1)}, bf16[256,1024]{1,0:T(8,128)(2,1)S(1)}, u32[]{:S(2)}, u32[]{:S(2)}) collective-permute-start(bf16[256,1024]{1,0:T(8,128)(2,1)S(1)} %constant_dynamic-update-slice_fusion.refs_1_), channel_id=1, source_target_pairs={{0,8},{1,65},{2,10},{3,67},{4,12},{5,69},{6,14},{7,71},{8,16},{9,7... | collective-permute-start | bytes 1572872 | tf_op jit(solution)/shard_map/ppermute | solution.py:193
  40.6 13.0 %collective-permute-start.1 = (bf16[2064,128]{1,0:T(8,128)(2,1)S(1)}, bf16[2064,128]{1,0:T(8,128)(2,1)S(1)}, u32[]{:S(2)}, u32[]{:S(2)}) collective-permute-start(bf16[2064,128]{1,0:T(8,128)(2,1)S(1)} %shard_map.83), channel_id=1, source_target_pairs={{0,2},{1,3},{2,4},{3,5},{4,6},{5,7},{8,10},{9,11},{10,12},{11,13},... | collective-permute-start | bytes 1585160 | tf_op jit(solution)/shard_map/ppermute | solution.py:268
  43.8 5.0 %collective-permute-start.10 = (bf16[256,1024]{1,0:T(8,128)(2,1)S(1)}, bf16[256,1024]{1,0:T(8,128)(2,1)S(1)}, u32[]{:S(2)}, u32[]{:S(2)}) collective-permute-start(bf16[256,1024]{1,0:T(8,128)(2,1)S(1)} %constant_dynamic-update-slice_fusion.refs_1_), channel_id=1, source_target_pairs={{0,1},{1,0},{2,3},{3,2},{4,5},{5,4},{6,7},{7,6},{8,9},{9,8},{10,11... | collective-permute-start | bytes 1572872 | tf_op jit(solution)/shard_map/ppermute | solution.py:197
  45.6 10.4 %collective-permute-start.19 = (bf16[256,1024]{1,0:T(8,128)(2,1)S(1)}, bf16[256,1024]{1,0:T(8,128)(2,1)S(1)}, u32[]{:S(2)}, u32[]{:S(2)}) collective-permute-start(bf16[256,1024]{1,0:T(8,128)(2,1)S(1)} %collective-permute-done.11.refs_2_), channel_id=1, source_target_pairs={{0,8},{1,65},{2,10},{3,67},{4,12},{5,69},{6,14},{7,71},{8,16},{9,7... | collective-permute-start | bytes 1572872 | tf_op jit(solution)/shard_map/ppermute | solution.py:193
  46.1 10.0 %collective-permute-start.12 = (bf16[256,1024]{1,0:T(8,128)(2,1)S(1)}, bf16[256,1024]{1,0:T(8,128)(2,1)S(1)}, u32[]{:S(2)}, u32[]{:S(2)}) collective-permute-start(bf16[256,1024]{1,0:T(8,128)(2,1)S(1)} %collective-permute-done.11.refs_2_), channel_id=1, source_target_pairs={{0,1},{1,0},{2,3},{3,2},{4,5},{5,4},{6,7},{7,6},{8,9},{9,8},{10,11... | collective-permute-start | bytes 1572872 | tf_op jit(solution)/shard_map/ppermute | solution.py:197
  48.5 8.0 %collective-permute-start.21 = (bf16[256,1024]{1,0:T(8,128)(2,1)S(1)}, bf16[256,1024]{1,0:T(8,128)(2,1)S(1)}, u32[]{:S(2)}, u32[]{:S(2)}) collective-permute-start(bf16[256,1024]{1,0:T(8,128)(2,1)S(1)} %collective-permute-done.17.refs_5_), channel_id=1, source_target_pairs={{0,56},{1,193},{2,58},{3,195},{4,60},{5,197},{6,62},{7,199},{8,0},... | collective-permute-start | bytes 1572872 | tf_op jit(solution)/shard_map/ppermute | solution.py:193
  48.8 24.8 %collective-permute-start.16 = (bf16[256,1024]{1,0:T(8,128)(2,1)S(1)}, bf16[256,1024]{1,0:T(8,128)(2,1)S(1)}, u32[]{:S(2)}, u32[]{:S(2)}) collective-permute-start(bf16[256,1024]{1,0:T(8,128)(2,1)S(1)} %collective-permute-done.15.refs_4_), channel_id=1, source_target_pairs={{0,1},{1,0},{2,3},{3,2},{4,5},{5,4},{6,7},{7,6},{8,9},{9,8},{10,11... | collective-permute-start | bytes 1572872 | tf_op jit(solution)/shard_map/ppermute | solution.py:197
  53.6 19.9 %collective-permute-start.18 = (bf16[256,1024]{1,0:T(8,128)(2,1)S(1)}, bf16[256,1024]{1,0:T(8,128)(2,1)S(1)}, u32[]{:S(2)}, u32[]{:S(2)}) collective-permute-start(bf16[256,1024]{1,0:T(8,128)(2,1)S(1)} %collective-permute-done.17.refs_5_), channel_id=1, source_target_pairs={{0,1},{1,0},{2,3},{3,2},{4,5},{5,4},{6,7},{7,6},{8,9},{9,8},{10,11... | collective-permute-start | bytes 1572872 | tf_op jit(solution)/shard_map/ppermute | solution.py:197
  55.9 17.6 %collective-permute-start.14 = (bf16[256,1024]{1,0:T(8,128)(2,1)S(1)}, bf16[256,1024]{1,0:T(8,128)(2,1)S(1)}, u32[]{:S(2)}, u32[]{:S(2)}) collective-permute-start(bf16[256,1024]{1,0:T(8,128)(2,1)S(1)} %collective-permute-done.13.refs_3_), channel_id=1, source_target_pairs={{0,1},{1,0},{2,3},{3,2},{4,5},{5,4},{6,7},{7,6},{8,9},{9,8},{10,11... | collective-permute-start | bytes 1572872 | tf_op jit(solution)/shard_map/ppermute | solution.py:197
  56.1 17.5 %collective-permute-start.20 = (bf16[256,1024]{1,0:T(8,128)(2,1)S(1)}, bf16[256,1024]{1,0:T(8,128)(2,1)S(1)}, u32[]{:S(2)}, u32[]{:S(2)}) collective-permute-start(bf16[256,1024]{1,0:T(8,128)(2,1)S(1)} %collective-permute-done.19.refs_6_), channel_id=1, source_target_pairs={{0,1},{1,0},{2,3},{3,2},{4,5},{5,4},{6,7},{7,6},{8,9},{9,8},{10,11... | collective-permute-start | bytes 1572872 | tf_op jit(solution)/shard_map/ppermute | solution.py:197
  56.5 17.0 %collective-permute-start.22 = (bf16[256,1024]{1,0:T(8,128)(2,1)S(1)}, bf16[256,1024]{1,0:T(8,128)(2,1)S(1)}, u32[]{:S(2)}, u32[]{:S(2)}) collective-permute-start(bf16[256,1024]{1,0:T(8,128)(2,1)S(1)} %collective-permute-done.21.refs_7_), channel_id=1, source_target_pairs={{0,1},{1,0},{2,3},{3,2},{4,5},{5,4},{6,7},{7,6},{8,9},{9,8},{10,11... | collective-permute-start | bytes 1572872 | tf_op jit(solution)/shard_map/ppermute | solution.py:197
  56.9 6.6 %copy-start.3 = (f32[2048]{0:T(1024)S(1)}, f32[2048]{0:T(1024)}, u32[]{:S(2)}) copy-start(f32[2048]{0:T(1024)} %param.14) | copy-start | bytes 24580

commit v3 on v2

--- a/solution.py
+++ b/solution.py
@@ -61,7 +61,7 @@
         pay_ref[pl.ds((step * STEP + i) * HEAD, HEAD)] = (parts[1] + fade * parts[0]).astype(BF16)
 
 
-def inner_kernel(rate_ref, u_ref, q_ref, k_ref, v_ref, mid_ref, out_ref, lag_ref, mask_ref, open_ref):
+def inner_kernel(base, rate_ref, u_ref, q_ref, k_ref, v_ref, mid_ref, out_ref, lag_ref, mask_ref, open_ref):
     step = pl.program_id(0)
 
     @pl.when(step == 0)
@@ -78,8 +78,8 @@
 
     past = (1 + lax.broadcasted_iota(jnp.int32, (HALF, HEAD), 0)).astype(F32)
     for i in range(STEP):
-        ld = log_decay(rate_ref, step * STEP + i)
-        decay = jnp.exp(lag_ref[...] * log_decay(rate_ref, step * STEP + i, HALF))
+        ld = log_decay(rate_ref, (base + step) * STEP + i)
+        decay = jnp.exp(lag_ref[...] * log_decay(rate_ref, (base + step) * STEP + i, HALF))
         cols = slice(i * HEAD, (i + 1) * HEAD)
         for b in range(2):
             rows = slice(b * HALF, (b + 1) * HALF)
@@ -107,7 +107,7 @@
     out_ref[WIDTH:] = own_ref[WIDTH:]
 
 
-def gate_kernel(rate_ref, u_ref, one_ref, two_ref, q_ref, part_ref, a_ref, gain_ref, out_ref, open_ref):
+def gate_kernel(rate_ref, u_ref, one_ref, two_ref, q_ref, part0_ref, part1_ref, a_ref, gain_ref, out_ref, open_ref):
     step = pl.program_id(0)
     u = u_ref[...]
 
@@ -129,7 +129,8 @@
         fade = jnp.exp(jnp.full((1, HEAD), ROWS * 1.0, F32) * ld) * far
         state = near * one_ref[rows].astype(F32) + fade * two_ref[rows].astype(F32)
         carried = jnp.dot(q_ref[:, cols], state.astype(BF16), preferred_element_type=F32)
-        kept = part_ref[:, cols] + carried * (jnp.exp(past * ld) * open_ref[...])
+        part = jnp.where(step < 2, part0_ref[:, cols], part1_ref[:, cols])
+        kept = part + carried * (jnp.exp(past * ld) * open_ref[...])
         mean = jnp.mean(kept, axis=1, keepdims=True)
         centred = kept - mean
         variance = jnp.mean(centred * centred, axis=1, keepdims=True)
@@ -237,6 +238,7 @@
 
 def local(queries, keys, values, gates, user_ids, forget_rate, norm_gain, w_out):
     q, k, v, a = (pltpu.with_memory_space_constraint(x[0], pltpu.HBM) for x in (queries, keys, values, gates))
+    user_ids, forget_rate = (pltpu.with_memory_space_constraint(x, pltpu.HBM) for x in (user_ids, forget_rate))
     gain = norm_gain.reshape(1, WIDTH)
     steps = HEADS // STEP
     smem = pl.BlockSpec(memory_space=pltpu.SMEM)
@@ -256,22 +258,37 @@
         [pltpu.VMEM((2, HALF, HEAD), F32)], 270 * 10**6, 5 * mb,
     )(forget_rate, user_ids, k, v)
     one = lax.ppermute(own, "hist", [(i, i + 1) for i in range(NH - 1)])
-    part = call(
-        inner_kernel, (steps,), [smem, users, block, block, block, heads], block,
-        shape((ROWS, WIDTH), F32),
-        [pltpu.VMEM((HALF, HALF), F32), pltpu.VMEM((2, HALF, HALF), F32), pltpu.VMEM((HALF, HEAD), F32)],
-        1200 * 10**6, 11 * mb,
-    )(forget_rate, user_ids, q, k, v, mid)
+    parts = []
+    for i in range(2):
+
+        def at(j, i=i):
+            return 0, 2 * i + j
+
+        half = pl.BlockSpec((ROWS, COLS), at)
+        mids = pl.BlockSpec((STEP, HEAD, HEAD), lambda j, i=i: (2 * i + j, 0, 0))
+        parts.append(
+            call(
+                functools.partial(inner_kernel, 2 * i), (2,), [smem, users, half, half, half, mids],
+                block, shape((ROWS, WIDTH // 2), F32),
+                [pltpu.VMEM((HALF, HALF), F32), pltpu.VMEM((2, HALF, HALF), F32), pltpu.VMEM((HALF, HEAD), F32)],
+                600 * 10**6, 6 * mb,
+            )(forget_rate, user_ids, q, k, v, mid)
+        )
     pair = call(
         pair_kernel, (1,), [smem, users, full, full], full, pay_shape, [], 10**6, 3 * mb // 2
     )(forget_rate, user_ids, own, one)
     two = lax.ppermute(pair, "hist", [(i, i + 2) for i in range(NH - 2)])
     gated = call(
         gate_kernel, (steps,),
-        [smem, users, full, full, block, block, block, pl.BlockSpec((1, COLS), lambda i: (0, i))],
+        [
+            smem, users, full, full, block,
+            pl.BlockSpec((ROWS, COLS), lambda i: (0, jnp.minimum(i, 1))),
+            pl.BlockSpec((ROWS, COLS), lambda i: (0, jnp.maximum(i - 2, 0))),
+            block, pl.BlockSpec((1, COLS), lambda i: (0, i)),
+        ],
         block, shape((ROWS, WIDTH), BF16), [pltpu.VMEM((ROWS, HEAD), F32)],
         300 * 10**6, 11 * mb,
-    )(forget_rate, user_ids, one, two, q, part, a, gain)
+    )(forget_rate, user_ids, one, two, q, *parts, a, gain)
 
     mixed = None
     for owner, got in enumerate((pieces, others)):

time: 77.9 us -> 78.1 us (level)
  Pallas kernels: 25.4 us -> 27.2 us
  local copies, waits for them, and re-layouts: 2.34 us -> 0.99 us
    pallas_call x2 -> x3, Pallas kernels: 12.7 us -> 14.4 us  [the longest x2 8.01 us: local(): call(functools.partial(inner_kernel, 2 * i), (2,), [smem, users, half, ha...]
    unnamed x14 -> x6, local copies, waits for them, and re-layouts: 2.32 us -> 0.98 us
  transfers between devices with their start and end apart: 23 -> 23, of which waited for: 8 -> 8; matrix products, arithmetic and copies ran while one was open for 0% -> 0% of each run, Pallas kernels for 28% -> 30%
where the time goes in v3:
time: 78.1 us; the launch traced here: 77.8 us
  starting transfers between devices  31.7 us (41%)
  Pallas kernels  27.2 us (35%)
  waiting for transfers between devices  17.6 us (23%)
  local copies, waits for them, and re-layouts  0.99 us (1%)
    ppermute x13, starting transfers between devices, send(): return lax.ppermute(x, BOTH, moves(*ways))  18.3 us
    ppermute x13, waiting for transfers between devices, send(): return lax.ppermute(x, BOTH, moves(*ways))  13.2 us
    pallas_call x2, Pallas kernels, local(): call(functools.partial(inner_kernel, 2 * i), (2,), [smem, users, half, ha...  8.01 us
    pallas_call x2, Pallas kernels, local(): call(functools.partial(project_kernel, owner), (2,), [pl.BlockSpec(memory...  7.79 us
    pallas_call x1, Pallas kernels, local(): call(gate_kernel, (steps,), [smem, users, full, full, block, pl.BlockSpec...  6.38 us
    ppermute x8, starting transfers between devices, swapped(): return lax.ppermute(x, BOTH, [(i, i ^ 1) for i in range(NY * NZ * NH)])  5.44 us
    ppermute x1, starting transfers between devices, local(): one = lax.ppermute(own, 'hist', [(i, i + 1) for i in range(NH - 1)])  4.79 us
    ppermute x1, waiting for transfers between devices, local(): two = lax.ppermute(pair, 'hist', [(i, i + 2) for i in range(NH - 2)])  4.42 us
  transfers between devices with their start and end apart: 23, of which 8 were waited for; matrix products, arithmetic and copies ran while one was open for 0% of the time, Pallas kernels for 30%

profile of v3, /device:TPU:1, one launch (start us, length us, event | category | flops | bytes accessed | tf_op | source)
XLA Modules:
  0.0 77.8 jit_solution(3623183565714249434)
XLA Ops:
  0.0 0.0 copy-start
  0.0 0.9 %copy-done = bf16[64,2048]{1,0:T(8,128)(2,1)S(1)} copy-done((bf16[64,2048]{1,0:T(8,128)(2,1)S(1)}, bf16[64,2048]{1,0:T(8,128)(2,1)}, u32[]{:S(2)}) %copy-start) | copy-done | bytes 262168
  1.0 2.5 %collective-permute-start.2 = (bf16[64,1024]{1,0:T(8,128)(2,1)S(1)}, bf16[64,1024]{1,0:T(8,128)(2,1)S(1)}, u32[]{:S(2)}, u32[]{:S(2)}) collective-permute-start(bf16[64,1024]{1,0:T(8,128)(2,1)S(1)} %constant_dynamic-slice_fusion), channel_id=1, source_target_pairs={{0,64},{1,9},{2,66},{3,11},{4,68},{5,13},{6,70},{7,15},{8,72},{9,1... | collective-permute-start | bytes 393224 | tf_op jit(solution)/shard_map/ppermute | solution.py:194
  3.5 4.0 %collective-permute-start.3 = (bf16[64,1024]{1,0:T(8,128)(2,1)S(1)}, bf16[64,1024]{1,0:T(8,128)(2,1)S(1)}, u32[]{:S(2)}, u32[]{:S(2)}) collective-permute-start(bf16[64,1024]{1,0:T(8,128)(2,1)S(1)} %constant_dynamic-slice_fusion), channel_id=1, source_target_pairs={{0,32},{1,57},{2,34},{3,59},{4,36},{5,61},{6,38},{7,63},{8,40},{9,... | collective-permute-start | bytes 393224 | tf_op jit(solution)/shard_map/ppermute | solution.py:194
  7.5 2.5 %collective-permute-done.2 = bf16[64,1024]{1,0:T(8,128)(2,1)S(1)} collective-permute-done((bf16[64,1024]{1,0:T(8,128)(2,1)S(1)}, bf16[64,1024]{1,0:T(8,128)(2,1)S(1)}, u32[]{:S(2)}, u32[]{:S(2)}) %collective-permute-start.2) | collective-permute-done | bytes 131104 | tf_op jit(solution)/shard_map/ppermute | solution.py:194
  10.0 0.0 collective-permute-start.6
  10.0 0.0 collective-permute-done.3
  10.0 2.8 %collective-permute-start.4 = (bf16[64,1024]{1,0:T(8,128)(2,1)S(1)}, bf16[64,1024]{1,0:T(8,128)(2,1)S(1)}, u32[]{:S(2)}, u32[]{:S(2)}) collective-permute-start(bf16[64,1024]{1,0:T(8,128)(2,1)S(1)} %collective-permute-done.3), channel_id=1, source_target_pairs={{0,64},{1,57},{2,66},{3,59},{4,68},{5,61},{6,70},{7,63},{8,72},{9,... | collective-permute-start | bytes 393224 | tf_op jit(solution)/shard_map/ppermute | solution.py:194
  12.8 3.5 %collective-permute-done.6 = bf16[64,1024]{1,0:T(8,128)(2,1)S(1)} collective-permute-done((bf16[64,1024]{1,0:T(8,128)(2,1)S(1)}, bf16[64,1024]{1,0:T(8,128)(2,1)S(1)}, u32[]{:S(2)}, u32[]{:S(2)}) %collective-permute-start.6) | collective-permute-done | bytes 131104 | tf_op jit(solution)/shard_map/ppermute | solution.py:194
  16.3 0.0 collective-permute-start.7
  16.3 4.0 %shard_map.82 = (bf16[2064,128]{1,0:T(8,128)(2,1)S(1)}, bf16[16,128,128]{2,1,0:T(8,128)(2,1)S(1)}) custom-call(f32[16]{0:T(128)} %rate_ref.9, s32[1,512]{1,0:T(1,128)} %u_ref.9, bf16[512,2048]{1,0:T(8,128)(2,1)} %bitcast.10, bf16[512,2048]{1,0:T(8,128)(2,1)} %bitcast.13), custom_call_target="tpu_custom_call" | custom-call | flops 270000000 | bytes 5242880 | tf_op jit(solution)/shard_map/pallas_call | solution.py:255
  20.3 4.8 %collective-permute-start = (bf16[2064,128]{1,0:T(8,128)(2,1)S(1)}, bf16[2064,128]{1,0:T(8,128)(2,1)S(1)}, u32[]{:S(2)}, u32[]{:S(2)}) collective-permute-start(bf16[2064,128]{1,0:T(8,128)(2,1)S(1)} %get-tuple-element.7.own_ref), channel_id=1, source_target_pairs={{0,1},{1,2},{2,3},{3,4},{4,5},{5,6},{6,7},{8,9},{9,10},{10,11},{11... | collective-permute-start | bytes 1585160 | tf_op jit(solution)/shard_map/ppermute | solution.py:260
  25.2 0.0 collective-permute-done.4
  25.2 4.3 %collective-permute-start.8 = (bf16[64,1024]{1,0:T(8,128)(2,1)S(1)}, bf16[64,1024]{1,0:T(8,128)(2,1)S(1)}, u32[]{:S(2)}, u32[]{:S(2)}) collective-permute-start(bf16[64,1024]{1,0:T(8,128)(2,1)S(1)} %collective-permute-done.4), channel_id=1, source_target_pairs={{0,64},{1,57},{2,66},{3,59},{4,68},{5,61},{6,70},{7,63},{8,72},{9,... | collective-permute-start | bytes 393224 | tf_op jit(solution)/shard_map/ppermute | solution.py:194
  29.4 0.0 collective-permute-done.7
  29.5 0.1 collective-permute-start.9
  29.6 0.1 collective-permute-start.11
  29.7 2.7 %collective-permute-start.15 = (bf16[256,1024]{1,0:T(8,128)(2,1)S(1)}, bf16[256,1024]{1,0:T(8,128)(2,1)S(1)}, u32[]{:S(2)}, u32[]{:S(2)}) collective-permute-start(bf16[256,1024]{1,0:T(8,128)(2,1)S(1)} %pad_maximum_fusion.refs_0_), channel_id=1, source_target_pairs={{0,56},{1,193},{2,58},{3,195},{4,60},{5,197},{6,62},{7,199},{8,0},... | collective-permute-start | bytes 1572872 | tf_op jit(solution)/shard_map/ppermute | solution.py:194
  32.4 0.0 collective-permute-done.8
  32.4 0.0 collective-permute-start.5
  32.4 3.9 %collective-permute-done.9 = bf16[64,1024]{1,0:T(8,128)(2,1)S(1)} collective-permute-done((bf16[64,1024]{1,0:T(8,128)(2,1)S(1)}, bf16[64,1024]{1,0:T(8,128)(2,1)S(1)}, u32[]{:S(2)}, u32[]{:S(2)}) %collective-permute-start.9) | collective-permute-done | bytes 131104 | tf_op jit(solution)/shard_map/ppermute | solution.py:194
  36.3 1.6 %collective-permute-start.17 = (bf16[256,1024]{1,0:T(8,128)(2,1)S(1)}, bf16[256,1024]{1,0:T(8,128)(2,1)S(1)}, u32[]{:S(2)}, u32[]{:S(2)}) collective-permute-start(bf16[256,1024]{1,0:T(8,128)(2,1)S(1)} %constant_dynamic-update-slice_fusion.refs_1_), channel_id=1, source_target_pairs={{0,56},{1,193},{2,58},{3,195},{4,60},{5,197},{6,62},{7,199},{8,0},... | collective-permute-start | bytes 1572872 | tf_op jit(solution)/shard_map/ppermute | solution.py:194
  37.9 0.0 collective-permute-done.one_ref
  37.9 0.0 collective-permute-start.13
  37.9 1.0 %shard_map.83 = bf16[2064,128]{1,0:T(8,128)(2,1)S(1)} custom-call(f32[16]{0:T(128)} %rate_ref.9, s32[1,512]{1,0:T(1,128)} %u_ref.9, bf16[2064,128]{1,0:T(8,128)(2,1)S(1)} %get-tuple-element.7.own_ref, bf16[2064,128]{1,0:T(8,128)(2,1)S(1)} %collective-permute-done.one_ref), custom_call_target="tpu_custom_call" | custom-call | flops 1000000 | bytes 1572864 | tf_op jit(solution)/shard_map/pallas_call | solution.py:277
  38.9 0.4 collective-permute-done.11.refs_2_
  39.3 3.1 %collective-permute-start.1 = (bf16[2064,128]{1,0:T(8,128)(2,1)S(1)}, bf16[2064,128]{1,0:T(8,128)(2,1)S(1)}, u32[]{:S(2)}, u32[]{:S(2)}) collective-permute-start(bf16[2064,128]{1,0:T(8,128)(2,1)S(1)} %shard_map.83), channel_id=1, source_target_pairs={{0,2},{1,3},{2,4},{3,5},{4,6},{5,7},{8,10},{9,11},{10,12},{11,13},... | collective-permute-start | bytes 1585160 | tf_op jit(solution)/shard_map/ppermute | solution.py:280
  42.4 0.0 collective-permute-done.15.refs_4_
  42.4 1.8 %collective-permute-start.10 = (bf16[256,1024]{1,0:T(8,128)(2,1)S(1)}, bf16[256,1024]{1,0:T(8,128)(2,1)S(1)}, u32[]{:S(2)}, u32[]{:S(2)}) collective-permute-start(bf16[256,1024]{1,0:T(8,128)(2,1)S(1)} %constant_dynamic-update-slice_fusion.refs_1_), channel_id=1, source_target_pairs={{0,1},{1,0},{2,3},{3,2},{4,5},{5,4},{6,7},{7,6},{8,9},{9,8},{10,11... | collective-permute-start | bytes 1572872 | tf_op jit(solution)/shard_map/ppermute | solution.py:198
  44.2 0.0 collective-permute-done.5.refs_0_
  44.2 0.0 collective-permute-start.19
  44.2 0.5 collective-permute-done.17.refs_5_
  44.7 0.0 collective-permute-start.12
  44.7 2.4 %collective-permute-done.13.refs_3_ = bf16[256,1024]{1,0:T(8,128)(2,1)S(1)} collective-permute-done((bf16[256,1024]{1,0:T(8,128)(2,1)S(1)}, bf16[256,1024]{1,0:T(8,128)(2,1)S(1)}, u32[]{:S(2)}, u32[]{:S(2)}) %collective-permute-start.13) | collective-permute-done | bytes 524320 | tf_op jit(solution)/shard_map/ppermute | solution.py:194
  47.1 0.3 collective-permute-start.21
  47.4 0.0 collective-permute-done.10.refs_1_
  47.4 0.4 collective-permute-start.16
  47.9 4.4 %collective-permute-done.1.two_ref = bf16[2064,128]{1,0:T(8,128)(2,1)S(1)} collective-permute-done((bf16[2064,128]{1,0:T(8,128)(2,1)S(1)}, bf16[2064,128]{1,0:T(8,128)(2,1)S(1)}, u32[]{:S(2)}, u32[]{:S(2)}) %collective-permute-start.1) | collective-permute-done | bytes 528416 | tf_op jit(solution)/shard_map/ppermute | solution.py:280
  52.3 2.3 %collective-permute-start.18 = (bf16[256,1024]{1,0:T(8,128)(2,1)S(1)}, bf16[256,1024]{1,0:T(8,128)(2,1)S(1)}, u32[]{:S(2)}, u32[]{:S(2)}) collective-permute-start(bf16[256,1024]{1,0:T(8,128)(2,1)S(1)} %collective-permute-done.17.refs_5_), channel_id=1, source_target_pairs={{0,1},{1,0},{2,3},{3,2},{4,5},{5,4},{6,7},{7,6},{8,9},{9,8},{10,11... | collective-permute-start | bytes 1572872 | tf_op jit(solution)/shard_map/ppermute | solution.py:198
  54.6 0.0 collective-permute-done.19.refs_6_
  54.6 0.1 collective-permute-start.14
  54.7 0.0 collective-permute-done.12.refs_2_
  54.7 0.4 collective-permute-start.20
  55.1 0.1 collective-permute-done.21.refs_7_
  55.2 0.4 collective-permute-start.22
  55.5 4.0 %shard_map.84.part0_ref = f32[512,1024]{1,0:T(8,128)S(1)} custom-call(f32[16]{0:T(128)} %rate_ref.9, s32[1,512]{1,0:T(1,128)} %u_ref.9, bf16[512,2048]{1,0:T(8,128)(2,1)} %bitcast.7, bf16[512,2048]{1,0:T(8,128)(2,1)} %bitcast.11, bf16[512,2048]{1,0:T(8,128)(2,1)} %bitcast.14, bf16[16,128,128]{2,1,0:T(8,128)(2,1)S(1)} %get-tuple-element.8.mid_ref), custom_call_target="tpu_custom_call" | custom-call | flops 600000000 | bytes 6291456 | tf_op jit(solution)/shard_map/pallas_call | solution.py:270
  59.5 0.0 copy-start.1
  59.6 4.0 %shard_map.85.part1_ref = f32[512,1024]{1,0:T(8,128)S(1)} custom-call(f32[16]{0:T(128)} %rate_ref.9, s32[1,512]{1,0:T(1,128)} %u_ref.9, bf16[512,2048]{1,0:T(8,128)(2,1)} %bitcast.8, bf16[512,2048]{1,0:T(8,128)(2,1)} %bitcast.12, bf16[512,2048]{1,0:T(8,128)(2,1)} %bitcast.15, bf16[16,128,128]{2,1,0:T(8,128)(2,1)S(1)} %get-tuple-element.8.mid_ref), custom_call_target="tpu_custom_call" | custom-call | flops 600000000 | bytes 6291456 | tf_op jit(solution)/shard_map/pallas_call | solution.py:270
  63.6 0.0 copy-done.1
  63.6 6.4 %shard_map.86.g_ref = bf16[512,2048]{1,0:T(8,128)(2,1)S(1)} custom-call(f32[16]{0:T(128)} %rate_ref.9, s32[1,512]{1,0:T(1,128)} %u_ref.9, bf16[2064,128]{1,0:T(8,128)(2,1)S(1)} %collective-permute-done.one_ref, bf16[2064,128]{1,0:T(8,128)(2,1)S(1)} %collective-permute-done.1.two_ref, bf16[512,2048]{1,0:T(8,128)(2,1)} %bitcast.9, ...), custom_call_target="tpu_custom_call" | custom-call | flops 300000000 | bytes 11534336 | tf_op jit(solution)/shard_map/pallas_call | solution.py:281
  70.0 3.9 %shard_map.87.refs_8_ = bf16[512,2048]{1,0:T(8,128)(2,1)} custom-call(bf16[512,2048]{1,0:T(8,128)(2,1)S(1)} %shard_map.86.g_ref, bf16[256,1024]{1,0:T(8,128)(2,1)S(1)} %pad_maximum_fusion.refs_0_, bf16[256,1024]{1,0:T(8,128)(2,1)S(1)} %constant_dynamic-update-slice_fusion.refs_1_, bf16[256,1024]{1,0:T(8,128)(2,1)S(1)} %collective-permute-done.11.refs_2_, ...), custom_call_target="tpu_custom_call" | custom-call | flops 2150000128 | bytes 7340032 | tf_op jit(solution)/shard_map/pallas_call | solution.py:300
  73.9 0.0 collective-permute-done.16.refs_4_
  73.9 0.0 collective-permute-done.14.refs_3_
  73.9 0.0 collective-permute-done.18.refs_5_
  73.9 0.0 collective-permute-done.20.refs_6_
  73.9 0.0 collective-permute-done.22.refs_7_
  73.9 3.9 %shard_map.88 = bf16[512,2048]{1,0:T(8,128)(2,1)} custom-call(bf16[512,2048]{1,0:T(8,128)(2,1)S(1)} %shard_map.86.g_ref, bf16[256,1024]{1,0:T(8,128)(2,1)S(1)} %collective-permute-done.5.refs_0_, bf16[256,1024]{1,0:T(8,128)(2,1)S(1)} %collective-permute-done.10.refs_1_, ...), custom_call_target="tpu_custom_call", output_to_operand_aliasing={{}: (9, {})} | custom-call | flops 2150000128 | bytes 7340032 | tf_op jit(solution)/shard_map/pallas_call | solution.py:300
  (6 shorter events, 0.1 us)
Async XLA Ops:
  0.0 1.0 %copy-start = (bf16[64,2048]{1,0:T(8,128)(2,1)S(1)}, bf16[64,2048]{1,0:T(8,128)(2,1)}, u32[]{:S(2)}) copy-start(bf16[64,2048]{1,0:T(8,128)(2,1)} %param.15) | copy-start | bytes 786436
  1.0 9.1 %collective-permute-start.2 = (bf16[64,1024]{1,0:T(8,128)(2,1)S(1)}, bf16[64,1024]{1,0:T(8,128)(2,1)S(1)}, u32[]{:S(2)}, u32[]{:S(2)}) collective-permute-start(bf16[64,1024]{1,0:T(8,128)(2,1)S(1)} %constant_dynamic-slice_fusion), channel_id=1, source_target_pairs={{0,64},{1,9},{2,66},{3,11},{4,68},{5,13},{6,70},{7,15},{8,72},{9,1... | collective-permute-start | bytes 393224 | tf_op jit(solution)/shard_map/ppermute | solution.py:194
  3.5 6.5 %collective-permute-start.3 = (bf16[64,1024]{1,0:T(8,128)(2,1)S(1)}, bf16[64,1024]{1,0:T(8,128)(2,1)S(1)}, u32[]{:S(2)}, u32[]{:S(2)}) collective-permute-start(bf16[64,1024]{1,0:T(8,128)(2,1)S(1)} %constant_dynamic-slice_fusion), channel_id=1, source_target_pairs={{0,32},{1,57},{2,34},{3,59},{4,36},{5,61},{6,38},{7,63},{8,40},{9,... | collective-permute-start | bytes 393224 | tf_op jit(solution)/shard_map/ppermute | solution.py:194
  10.0 6.3 %collective-permute-start.6 = (bf16[64,1024]{1,0:T(8,128)(2,1)S(1)}, bf16[64,1024]{1,0:T(8,128)(2,1)S(1)}, u32[]{:S(2)}, u32[]{:S(2)}) collective-permute-start(bf16[64,1024]{1,0:T(8,128)(2,1)S(1)} %collective-permute-done.2), channel_id=1, source_target_pairs={{0,64},{1,9},{2,66},{3,11},{4,68},{5,13},{6,70},{7,15},{8,72},{9,1... | collective-permute-start | bytes 393224 | tf_op jit(solution)/shard_map/ppermute | solution.py:194
  10.0 15.1 %collective-permute-start.4 = (bf16[64,1024]{1,0:T(8,128)(2,1)S(1)}, bf16[64,1024]{1,0:T(8,128)(2,1)S(1)}, u32[]{:S(2)}, u32[]{:S(2)}) collective-permute-start(bf16[64,1024]{1,0:T(8,128)(2,1)S(1)} %collective-permute-done.3), channel_id=1, source_target_pairs={{0,64},{1,57},{2,66},{3,59},{4,68},{5,61},{6,70},{7,63},{8,72},{9,... | collective-permute-start | bytes 393224 | tf_op jit(solution)/shard_map/ppermute | solution.py:194
  16.3 13.1 %collective-permute-start.7 = (bf16[64,1024]{1,0:T(8,128)(2,1)S(1)}, bf16[64,1024]{1,0:T(8,128)(2,1)S(1)}, u32[]{:S(2)}, u32[]{:S(2)}) collective-permute-start(bf16[64,1024]{1,0:T(8,128)(2,1)S(1)} %collective-permute-done.6), channel_id=1, source_target_pairs={{0,64},{1,9},{2,66},{3,11},{4,68},{5,13},{6,70},{7,15},{8,72},{9,1... | collective-permute-start | bytes 393224 | tf_op jit(solution)/shard_map/ppermute | solution.py:194
  20.3 17.5 %collective-permute-start = (bf16[2064,128]{1,0:T(8,128)(2,1)S(1)}, bf16[2064,128]{1,0:T(8,128)(2,1)S(1)}, u32[]{:S(2)}, u32[]{:S(2)}) collective-permute-start(bf16[2064,128]{1,0:T(8,128)(2,1)S(1)} %get-tuple-element.7.own_ref), channel_id=1, source_target_pairs={{0,1},{1,2},{2,3},{3,4},{4,5},{5,6},{6,7},{8,9},{9,10},{10,11},{11... | collective-permute-start | bytes 1585160 | tf_op jit(solution)/shard_map/ppermute | solution.py:260
  25.2 7.2 %collective-permute-start.8 = (bf16[64,1024]{1,0:T(8,128)(2,1)S(1)}, bf16[64,1024]{1,0:T(8,128)(2,1)S(1)}, u32[]{:S(2)}, u32[]{:S(2)}) collective-permute-start(bf16[64,1024]{1,0:T(8,128)(2,1)S(1)} %collective-permute-done.4), channel_id=1, source_target_pairs={{0,64},{1,57},{2,66},{3,59},{4,68},{5,61},{6,70},{7,63},{8,72},{9,... | collective-permute-start | bytes 393224 | tf_op jit(solution)/shard_map/ppermute | solution.py:194
  29.5 6.8 %collective-permute-start.9 = (bf16[64,1024]{1,0:T(8,128)(2,1)S(1)}, bf16[64,1024]{1,0:T(8,128)(2,1)S(1)}, u32[]{:S(2)}, u32[]{:S(2)}) collective-permute-start(bf16[64,1024]{1,0:T(8,128)(2,1)S(1)} %get-tuple-element.9), channel_id=1, source_target_pairs={{0,192},{1,9},{2,194},{3,11},{4,196},{5,13},{6,198},{7,15},{8,200}... | collective-permute-start | bytes 393224 | tf_op jit(solution)/shard_map/ppermute | solution.py:194
  29.6 9.6 %collective-permute-start.11 = (bf16[256,1024]{1,0:T(8,128)(2,1)S(1)}, bf16[256,1024]{1,0:T(8,128)(2,1)S(1)}, u32[]{:S(2)}, u32[]{:S(2)}) collective-permute-start(bf16[256,1024]{1,0:T(8,128)(2,1)S(1)} %pad_maximum_fusion.refs_0_), channel_id=1, source_target_pairs={{0,8},{1,65},{2,10},{3,67},{4,12},{5,69},{6,14},{7,71},{8,16},{9,7... | collective-permute-start | bytes 1572872 | tf_op jit(solution)/shard_map/ppermute | solution.py:194
  29.7 12.7 %collective-permute-start.15 = (bf16[256,1024]{1,0:T(8,128)(2,1)S(1)}, bf16[256,1024]{1,0:T(8,128)(2,1)S(1)}, u32[]{:S(2)}, u32[]{:S(2)}) collective-permute-start(bf16[256,1024]{1,0:T(8,128)(2,1)S(1)} %pad_maximum_fusion.refs_0_), channel_id=1, source_target_pairs={{0,56},{1,193},{2,58},{3,195},{4,60},{5,197},{6,62},{7,199},{8,0},... | collective-permute-start | bytes 1572872 | tf_op jit(solution)/shard_map/ppermute | solution.py:194
  32.4 11.8 %collective-permute-start.5 = (bf16[256,1024]{1,0:T(8,128)(2,1)S(1)}, bf16[256,1024]{1,0:T(8,128)(2,1)S(1)}, u32[]{:S(2)}, u32[]{:S(2)}) collective-permute-start(bf16[256,1024]{1,0:T(8,128)(2,1)S(1)} %pad_maximum_fusion.refs_0_), channel_id=1, source_target_pairs={{0,1},{1,0},{2,3},{3,2},{4,5},{5,4},{6,7},{7,6},{8,9},{9,8},{10,11... | collective-permute-start | bytes 1572872 | tf_op jit(solution)/shard_map/ppermute | solution.py:198
  36.3 8.4 %collective-permute-start.17 = (bf16[256,1024]{1,0:T(8,128)(2,1)S(1)}, bf16[256,1024]{1,0:T(8,128)(2,1)S(1)}, u32[]{:S(2)}, u32[]{:S(2)}) collective-permute-start(bf16[256,1024]{1,0:T(8,128)(2,1)S(1)} %constant_dynamic-update-slice_fusion.refs_1_), channel_id=1, source_target_pairs={{0,56},{1,193},{2,58},{3,195},{4,60},{5,197},{6,62},{7,199},{8,0},... | collective-permute-start | bytes 1572872 | tf_op jit(solution)/shard_map/ppermute | solution.py:194
  37.9 9.2 %collective-permute-start.13 = (bf16[256,1024]{1,0:T(8,128)(2,1)S(1)}, bf16[256,1024]{1,0:T(8,128)(2,1)S(1)}, u32[]{:S(2)}, u32[]{:S(2)}) collective-permute-start(bf16[256,1024]{1,0:T(8,128)(2,1)S(1)} %constant_dynamic-update-slice_fusion.refs_1_), channel_id=1, source_target_pairs={{0,8},{1,65},{2,10},{3,67},{4,12},{5,69},{6,14},{7,71},{8,16},{9,7... | collective-permute-start | bytes 1572872 | tf_op jit(solution)/shard_map/ppermute | solution.py:194
  39.3 13.0 %collective-permute-start.1 = (bf16[2064,128]{1,0:T(8,128)(2,1)S(1)}, bf16[2064,128]{1,0:T(8,128)(2,1)S(1)}, u32[]{:S(2)}, u32[]{:S(2)}) collective-permute-start(bf16[2064,128]{1,0:T(8,128)(2,1)S(1)} %shard_map.83), channel_id=1, source_target_pairs={{0,2},{1,3},{2,4},{3,5},{4,6},{5,7},{8,10},{9,11},{10,12},{11,13},... | collective-permute-start | bytes 1585160 | tf_op jit(solution)/shard_map/ppermute | solution.py:280
  42.4 5.0 %collective-permute-start.10 = (bf16[256,1024]{1,0:T(8,128)(2,1)S(1)}, bf16[256,1024]{1,0:T(8,128)(2,1)S(1)}, u32[]{:S(2)}, u32[]{:S(2)}) collective-permute-start(bf16[256,1024]{1,0:T(8,128)(2,1)S(1)} %constant_dynamic-update-slice_fusion.refs_1_), channel_id=1, source_target_pairs={{0,1},{1,0},{2,3},{3,2},{4,5},{5,4},{6,7},{7,6},{8,9},{9,8},{10,11... | collective-permute-start | bytes 1572872 | tf_op jit(solution)/shard_map/ppermute | solution.py:198
  44.2 10.4 %collective-permute-start.19 = (bf16[256,1024]{1,0:T(8,128)(2,1)S(1)}, bf16[256,1024]{1,0:T(8,128)(2,1)S(1)}, u32[]{:S(2)}, u32[]{:S(2)}) collective-permute-start(bf16[256,1024]{1,0:T(8,128)(2,1)S(1)} %collective-permute-done.11.refs_2_), channel_id=1, source_target_pairs={{0,8},{1,65},{2,10},{3,67},{4,12},{5,69},{6,14},{7,71},{8,16},{9,7... | collective-permute-start | bytes 1572872 | tf_op jit(solution)/shard_map/ppermute | solution.py:194
  44.7 10.0 %collective-permute-start.12 = (bf16[256,1024]{1,0:T(8,128)(2,1)S(1)}, bf16[256,1024]{1,0:T(8,128)(2,1)S(1)}, u32[]{:S(2)}, u32[]{:S(2)}) collective-permute-start(bf16[256,1024]{1,0:T(8,128)(2,1)S(1)} %collective-permute-done.11.refs_2_), channel_id=1, source_target_pairs={{0,1},{1,0},{2,3},{3,2},{4,5},{5,4},{6,7},{7,6},{8,9},{9,8},{10,11... | collective-permute-start | bytes 1572872 | tf_op jit(solution)/shard_map/ppermute | solution.py:198
  47.1 8.0 %collective-permute-start.21 = (bf16[256,1024]{1,0:T(8,128)(2,1)S(1)}, bf16[256,1024]{1,0:T(8,128)(2,1)S(1)}, u32[]{:S(2)}, u32[]{:S(2)}) collective-permute-start(bf16[256,1024]{1,0:T(8,128)(2,1)S(1)} %collective-permute-done.17.refs_5_), channel_id=1, source_target_pairs={{0,56},{1,193},{2,58},{3,195},{4,60},{5,197},{6,62},{7,199},{8,0},... | collective-permute-start | bytes 1572872 | tf_op jit(solution)/shard_map/ppermute | solution.py:194
  47.4 26.5 %collective-permute-start.16 = (bf16[256,1024]{1,0:T(8,128)(2,1)S(1)}, bf16[256,1024]{1,0:T(8,128)(2,1)S(1)}, u32[]{:S(2)}, u32[]{:S(2)}) collective-permute-start(bf16[256,1024]{1,0:T(8,128)(2,1)S(1)} %collective-permute-done.15.refs_4_), channel_id=1, source_target_pairs={{0,1},{1,0},{2,3},{3,2},{4,5},{5,4},{6,7},{7,6},{8,9},{9,8},{10,11... | collective-permute-start | bytes 1572872 | tf_op jit(solution)/shard_map/ppermute | solution.py:198
  52.3 21.6 %collective-permute-start.18 = (bf16[256,1024]{1,0:T(8,128)(2,1)S(1)}, bf16[256,1024]{1,0:T(8,128)(2,1)S(1)}, u32[]{:S(2)}, u32[]{:S(2)}) collective-permute-start(bf16[256,1024]{1,0:T(8,128)(2,1)S(1)} %collective-permute-done.17.refs_5_), channel_id=1, source_target_pairs={{0,1},{1,0},{2,3},{3,2},{4,5},{5,4},{6,7},{7,6},{8,9},{9,8},{10,11... | collective-permute-start | bytes 1572872 | tf_op jit(solution)/shard_map/ppermute | solution.py:198
  54.6 19.3 %collective-permute-start.14 = (bf16[256,1024]{1,0:T(8,128)(2,1)S(1)}, bf16[256,1024]{1,0:T(8,128)(2,1)S(1)}, u32[]{:S(2)}, u32[]{:S(2)}) collective-permute-start(bf16[256,1024]{1,0:T(8,128)(2,1)S(1)} %collective-permute-done.13.refs_3_), channel_id=1, source_target_pairs={{0,1},{1,0},{2,3},{3,2},{4,5},{5,4},{6,7},{7,6},{8,9},{9,8},{10,11... | collective-permute-start | bytes 1572872 | tf_op jit(solution)/shard_map/ppermute | solution.py:198
  54.7 19.2 %collective-permute-start.20 = (bf16[256,1024]{1,0:T(8,128)(2,1)S(1)}, bf16[256,1024]{1,0:T(8,128)(2,1)S(1)}, u32[]{:S(2)}, u32[]{:S(2)}) collective-permute-start(bf16[256,1024]{1,0:T(8,128)(2,1)S(1)} %collective-permute-done.19.refs_6_), channel_id=1, source_target_pairs={{0,1},{1,0},{2,3},{3,2},{4,5},{5,4},{6,7},{7,6},{8,9},{9,8},{10,11... | collective-permute-start | bytes 1572872 | tf_op jit(solution)/shard_map/ppermute | solution.py:198
  55.2 18.7 %collective-permute-start.22 = (bf16[256,1024]{1,0:T(8,128)(2,1)S(1)}, bf16[256,1024]{1,0:T(8,128)(2,1)S(1)}, u32[]{:S(2)}, u32[]{:S(2)}) collective-permute-start(bf16[256,1024]{1,0:T(8,128)(2,1)S(1)} %collective-permute-done.21.refs_7_), channel_id=1, source_target_pairs={{0,1},{1,0},{2,3},{3,2},{4,5},{5,4},{6,7},{7,6},{8,9},{9,8},{10,11... | collective-permute-start | bytes 1572872 | tf_op jit(solution)/shard_map/ppermute | solution.py:198
  59.5 4.0 %copy-start.1 = (f32[2048]{0:T(1024)S(1)}, f32[2048]{0:T(1024)}, u32[]{:S(2)}) copy-start(f32[2048]{0:T(1024)} %param.14) | copy-start | bytes 24580

commit v4 on v3

--- a/solution.py
+++ b/solution.py
@@ -129,7 +129,8 @@
         fade = jnp.exp(jnp.full((1, HEAD), ROWS * 1.0, F32) * ld) * far
         state = near * one_ref[rows].astype(F32) + fade * two_ref[rows].astype(F32)
         carried = jnp.dot(q_ref[:, cols], state.astype(BF16), preferred_element_type=F32)
-        part = jnp.where(step < 2, part0_ref[:, cols], part1_ref[:, cols])
+        here = pl.ds(pl.multiple_of((step % 2) * COLS + i * HEAD, HEAD), HEAD)
+        part = jnp.where(step < 2, part0_ref[:, here], part1_ref[:, here])
         kept = part + carried * (jnp.exp(past * ld) * open_ref[...])
         mean = jnp.mean(kept, axis=1, keepdims=True)
         centred = kept - mean
@@ -246,6 +247,7 @@
     block = pl.BlockSpec((ROWS, COLS), lambda i: (0, i))
     heads = pl.BlockSpec((STEP, HEAD, HEAD), lambda i: (i, 0, 0))
     full = pl.BlockSpec((PAYLOAD, HEAD), lambda i: (0, 0))
+    vmem = pl.BlockSpec(memory_space=pltpu.VMEM)
     shape = jax.ShapeDtypeStruct
     pay_shape = shape((PAYLOAD, HEAD), BF16)
     mb = 1 << 20
@@ -275,16 +277,13 @@
             )(forget_rate, user_ids, q, k, v, mid)
         )
     pair = call(
-        pair_kernel, (1,), [smem, users, full, full], full, pay_shape, [], 10**6, 3 * mb // 2
+        pair_kernel, (1,), [smem, users, vmem, vmem], vmem, pay_shape, [], 10**6, 3 * mb // 2
     )(forget_rate, user_ids, own, one)
     two = lax.ppermute(pair, "hist", [(i, i + 2) for i in range(NH - 2)])
     gated = call(
         gate_kernel, (steps,),
         [
-            smem, users, full, full, block,
-            pl.BlockSpec((ROWS, COLS), lambda i: (0, jnp.minimum(i, 1))),
-            pl.BlockSpec((ROWS, COLS), lambda i: (0, jnp.maximum(i - 2, 0))),
-            block, pl.BlockSpec((1, COLS), lambda i: (0, i)),
+            smem, users, vmem, vmem, block, vmem, vmem, block, pl.BlockSpec((1, COLS), lambda i: (0, i)),
         ],
         block, shape((ROWS, WIDTH), BF16), [pltpu.VMEM((ROWS, HEAD), F32)],
         300 * 10**6, 11 * mb,

time: 78.1 us -> 78.3 us (level)
  no operation moved by 1% of the time
where the time goes in v4:
time: 78.3 us; the launch traced here: 78 us
  starting transfers between devices  31.7 us (40%)
  Pallas kernels  27.4 us (35%)
  waiting for transfers between devices  17.6 us (22%)
  local copies, waits for them, and re-layouts  0.99 us (1%)
    ppermute x13, starting transfers between devices, send(): return lax.ppermute(x, BOTH, moves(*ways))  18.3 us
    ppermute x13, waiting for transfers between devices, send(): return lax.ppermute(x, BOTH, moves(*ways))  13.2 us
    pallas_call x2, Pallas kernels, local(): call(functools.partial(inner_kernel, 2 * i), (2,), [smem, users, half, ha...  8.01 us
    pallas_call x2, Pallas kernels, local(): call(functools.partial(project_kernel, owner), (2,), [pl.BlockSpec(memory...  7.79 us
    pallas_call x1, Pallas kernels, local(): call(gate_kernel, (steps,), [smem, users, vmem, vmem, block, vmem, vmem,...  6.58 us
    ppermute x8, starting transfers between devices, swapped(): return lax.ppermute(x, BOTH, [(i, i ^ 1) for i in range(NY * NZ * NH)])  5.44 us
    ppermute x1, starting transfers between devices, local(): one = lax.ppermute(own, 'hist', [(i, i + 1) for i in range(NH - 1)])  4.79 us
    ppermute x1, waiting for transfers between devices, local(): two = lax.ppermute(pair, 'hist', [(i, i + 2) for i in range(NH - 2)])  4.42 us
  transfers between devices with their start and end apart: 23, of which 8 were waited for; matrix products, arithmetic and copies ran while one was open for 0% of the time, Pallas kernels for 30%

profile of v4, /device:TPU:1, one launch (start us, length us, event | category | flops | bytes accessed | tf_op | source)
XLA Modules:
  0.0 78.0 jit_solution(3407283478339921289)
XLA Ops:
  0.0 0.0 copy-start
  0.0 0.9 %copy-done = bf16[64,2048]{1,0:T(8,128)(2,1)S(1)} copy-done((bf16[64,2048]{1,0:T(8,128)(2,1)S(1)}, bf16[64,2048]{1,0:T(8,128)(2,1)}, u32[]{:S(2)}) %copy-start) | copy-done | bytes 262168
  1.0 2.5 %collective-permute-start.2 = (bf16[64,1024]{1,0:T(8,128)(2,1)S(1)}, bf16[64,1024]{1,0:T(8,128)(2,1)S(1)}, u32[]{:S(2)}, u32[]{:S(2)}) collective-permute-start(bf16[64,1024]{1,0:T(8,128)(2,1)S(1)} %constant_dynamic-slice_fusion), channel_id=1, source_target_pairs={{0,64},{1,9},{2,66},{3,11},{4,68},{5,13},{6,70},{7,15},{8,72},{9,1... | collective-permute-start | bytes 393224 | tf_op jit(solution)/shard_map/ppermute | solution.py:195
  3.5 4.0 %collective-permute-start.3 = (bf16[64,1024]{1,0:T(8,128)(2,1)S(1)}, bf16[64,1024]{1,0:T(8,128)(2,1)S(1)}, u32[]{:S(2)}, u32[]{:S(2)}) collective-permute-start(bf16[64,1024]{1,0:T(8,128)(2,1)S(1)} %constant_dynamic-slice_fusion), channel_id=1, source_target_pairs={{0,32},{1,57},{2,34},{3,59},{4,36},{5,61},{6,38},{7,63},{8,40},{9,... | collective-permute-start | bytes 393224 | tf_op jit(solution)/shard_map/ppermute | solution.py:195
  7.5 2.5 %collective-permute-done.2 = bf16[64,1024]{1,0:T(8,128)(2,1)S(1)} collective-permute-done((bf16[64,1024]{1,0:T(8,128)(2,1)S(1)}, bf16[64,1024]{1,0:T(8,128)(2,1)S(1)}, u32[]{:S(2)}, u32[]{:S(2)}) %collective-permute-start.2) | collective-permute-done | bytes 131104 | tf_op jit(solution)/shard_map/ppermute | solution.py:195
  10.0 0.0 collective-permute-start.6
  10.0 0.0 collective-permute-done.3
  10.0 2.8 %collective-permute-start.4 = (bf16[64,1024]{1,0:T(8,128)(2,1)S(1)}, bf16[64,1024]{1,0:T(8,128)(2,1)S(1)}, u32[]{:S(2)}, u32[]{:S(2)}) collective-permute-start(bf16[64,1024]{1,0:T(8,128)(2,1)S(1)} %collective-permute-done.3), channel_id=1, source_target_pairs={{0,64},{1,57},{2,66},{3,59},{4,68},{5,61},{6,70},{7,63},{8,72},{9,... | collective-permute-start | bytes 393224 | tf_op jit(solution)/shard_map/ppermute | solution.py:195
  12.8 3.5 %collective-permute-done.6 = bf16[64,1024]{1,0:T(8,128)(2,1)S(1)} collective-permute-done((bf16[64,1024]{1,0:T(8,128)(2,1)S(1)}, bf16[64,1024]{1,0:T(8,128)(2,1)S(1)}, u32[]{:S(2)}, u32[]{:S(2)}) %collective-permute-start.6) | collective-permute-done | bytes 131104 | tf_op jit(solution)/shard_map/ppermute | solution.py:195
  16.3 0.0 collective-permute-start.7
  16.3 4.0 %shard_map.82 = (bf16[2064,128]{1,0:T(8,128)(2,1)S(1)}, bf16[16,128,128]{2,1,0:T(8,128)(2,1)S(1)}) custom-call(f32[16]{0:T(128)} %rate_ref.9, s32[1,512]{1,0:T(1,128)} %u_ref.9, bf16[512,2048]{1,0:T(8,128)(2,1)} %bitcast.10, bf16[512,2048]{1,0:T(8,128)(2,1)} %bitcast.13), custom_call_target="tpu_custom_call" | custom-call | flops 270000000 | bytes 5242880 | tf_op jit(solution)/shard_map/pallas_call | solution.py:257
  20.3 4.8 %collective-permute-start = (bf16[2064,128]{1,0:T(8,128)(2,1)S(1)}, bf16[2064,128]{1,0:T(8,128)(2,1)S(1)}, u32[]{:S(2)}, u32[]{:S(2)}) collective-permute-start(bf16[2064,128]{1,0:T(8,128)(2,1)S(1)} %get-tuple-element.7.own_ref), channel_id=1, source_target_pairs={{0,1},{1,2},{2,3},{3,4},{4,5},{5,6},{6,7},{8,9},{9,10},{10,11},{11... | collective-permute-start | bytes 1585160 | tf_op jit(solution)/shard_map/ppermute | solution.py:262
  25.2 0.0 collective-permute-done.4
  25.2 4.3 %collective-permute-start.8 = (bf16[64,1024]{1,0:T(8,128)(2,1)S(1)}, bf16[64,1024]{1,0:T(8,128)(2,1)S(1)}, u32[]{:S(2)}, u32[]{:S(2)}) collective-permute-start(bf16[64,1024]{1,0:T(8,128)(2,1)S(1)} %collective-permute-done.4), channel_id=1, source_target_pairs={{0,64},{1,57},{2,66},{3,59},{4,68},{5,61},{6,70},{7,63},{8,72},{9,... | collective-permute-start | bytes 393224 | tf_op jit(solution)/shard_map/ppermute | solution.py:195
  29.4 0.0 collective-permute-done.7
  29.5 0.1 collective-permute-start.9
  29.6 0.1 collective-permute-start.11
  29.7 2.7 %collective-permute-start.15 = (bf16[256,1024]{1,0:T(8,128)(2,1)S(1)}, bf16[256,1024]{1,0:T(8,128)(2,1)S(1)}, u32[]{:S(2)}, u32[]{:S(2)}) collective-permute-start(bf16[256,1024]{1,0:T(8,128)(2,1)S(1)} %pad_maximum_fusion.refs_0_), channel_id=1, source_target_pairs={{0,56},{1,193},{2,58},{3,195},{4,60},{5,197},{6,62},{7,199},{8,0},... | collective-permute-start | bytes 1572872 | tf_op jit(solution)/shard_map/ppermute | solution.py:195
  32.4 0.0 collective-permute-done.8
  32.4 0.0 collective-permute-start.5
  32.4 3.9 %collective-permute-done.9 = bf16[64,1024]{1,0:T(8,128)(2,1)S(1)} collective-permute-done((bf16[64,1024]{1,0:T(8,128)(2,1)S(1)}, bf16[64,1024]{1,0:T(8,128)(2,1)S(1)}, u32[]{:S(2)}, u32[]{:S(2)}) %collective-permute-start.9) | collective-permute-done | bytes 131104 | tf_op jit(solution)/shard_map/ppermute | solution.py:195
  36.3 1.6 %collective-permute-start.17 = (bf16[256,1024]{1,0:T(8,128)(2,1)S(1)}, bf16[256,1024]{1,0:T(8,128)(2,1)S(1)}, u32[]{:S(2)}, u32[]{:S(2)}) collective-permute-start(bf16[256,1024]{1,0:T(8,128)(2,1)S(1)} %constant_dynamic-update-slice_fusion.refs_1_), channel_id=1, source_target_pairs={{0,56},{1,193},{2,58},{3,195},{4,60},{5,197},{6,62},{7,199},{8,0},... | collective-permute-start | bytes 1572872 | tf_op jit(solution)/shard_map/ppermute | solution.py:195
  37.9 0.0 collective-permute-done.one_ref
  37.9 0.0 collective-permute-start.13
  37.9 1.0 %shard_map.83 = bf16[2064,128]{1,0:T(8,128)(2,1)S(1)} custom-call(f32[16]{0:T(128)} %rate_ref.9, s32[1,512]{1,0:T(1,128)} %u_ref.9, bf16[2064,128]{1,0:T(8,128)(2,1)S(1)} %get-tuple-element.7.own_ref, bf16[2064,128]{1,0:T(8,128)(2,1)S(1)} %collective-permute-done.one_ref), custom_call_target="tpu_custom_call" | custom-call | flops 1000000 | bytes 1572864 | tf_op jit(solution)/shard_map/pallas_call | solution.py:279
  38.9 0.4 collective-permute-done.11.refs_2_
  39.3 3.1 %collective-permute-start.1 = (bf16[2064,128]{1,0:T(8,128)(2,1)S(1)}, bf16[2064,128]{1,0:T(8,128)(2,1)S(1)}, u32[]{:S(2)}, u32[]{:S(2)}) collective-permute-start(bf16[2064,128]{1,0:T(8,128)(2,1)S(1)} %shard_map.83), channel_id=1, source_target_pairs={{0,2},{1,3},{2,4},{3,5},{4,6},{5,7},{8,10},{9,11},{10,12},{11,13},... | collective-permute-start | bytes 1585160 | tf_op jit(solution)/shard_map/ppermute | solution.py:282
  42.4 0.0 collective-permute-done.15.refs_4_
  42.4 1.8 %collective-permute-start.10 = (bf16[256,1024]{1,0:T(8,128)(2,1)S(1)}, bf16[256,1024]{1,0:T(8,128)(2,1)S(1)}, u32[]{:S(2)}, u32[]{:S(2)}) collective-permute-start(bf16[256,1024]{1,0:T(8,128)(2,1)S(1)} %constant_dynamic-update-slice_fusion.refs_1_), channel_id=1, source_target_pairs={{0,1},{1,0},{2,3},{3,2},{4,5},{5,4},{6,7},{7,6},{8,9},{9,8},{10,11... | collective-permute-start | bytes 1572872 | tf_op jit(solution)/shard_map/ppermute | solution.py:199
  44.2 0.0 collective-permute-done.5.refs_0_
  44.2 0.0 collective-permute-start.19
  44.2 0.5 collective-permute-done.17.refs_5_
  44.7 0.0 collective-permute-start.12
  44.7 2.4 %collective-permute-done.13.refs_3_ = bf16[256,1024]{1,0:T(8,128)(2,1)S(1)} collective-permute-done((bf16[256,1024]{1,0:T(8,128)(2,1)S(1)}, bf16[256,1024]{1,0:T(8,128)(2,1)S(1)}, u32[]{:S(2)}, u32[]{:S(2)}) %collective-permute-start.13) | collective-permute-done | bytes 524320 | tf_op jit(solution)/shard_map/ppermute | solution.py:195
  47.1 0.3 collective-permute-start.21
  47.4 0.0 collective-permute-done.10.refs_1_
  47.4 0.4 collective-permute-start.16
  47.9 4.4 %collective-permute-done.1.two_ref = bf16[2064,128]{1,0:T(8,128)(2,1)S(1)} collective-permute-done((bf16[2064,128]{1,0:T(8,128)(2,1)S(1)}, bf16[2064,128]{1,0:T(8,128)(2,1)S(1)}, u32[]{:S(2)}, u32[]{:S(2)}) %collective-permute-start.1) | collective-permute-done | bytes 528416 | tf_op jit(solution)/shard_map/ppermute | solution.py:282
  52.3 2.3 %collective-permute-start.18 = (bf16[256,1024]{1,0:T(8,128)(2,1)S(1)}, bf16[256,1024]{1,0:T(8,128)(2,1)S(1)}, u32[]{:S(2)}, u32[]{:S(2)}) collective-permute-start(bf16[256,1024]{1,0:T(8,128)(2,1)S(1)} %collective-permute-done.17.refs_5_), channel_id=1, source_target_pairs={{0,1},{1,0},{2,3},{3,2},{4,5},{5,4},{6,7},{7,6},{8,9},{9,8},{10,11... | collective-permute-start | bytes 1572872 | tf_op jit(solution)/shard_map/ppermute | solution.py:199
  54.6 0.0 collective-permute-done.19.refs_6_
  54.6 0.1 collective-permute-start.14
  54.7 0.0 collective-permute-done.12.refs_2_
  54.7 0.4 collective-permute-start.20
  55.1 0.1 collective-permute-done.21.refs_7_
  55.2 0.4 collective-permute-start.22
  55.5 4.0 %shard_map.84.part0_ref = f32[512,1024]{1,0:T(8,128)S(1)} custom-call(f32[16]{0:T(128)} %rate_ref.9, s32[1,512]{1,0:T(1,128)} %u_ref.9, bf16[512,2048]{1,0:T(8,128)(2,1)} %bitcast.7, bf16[512,2048]{1,0:T(8,128)(2,1)} %bitcast.11, bf16[512,2048]{1,0:T(8,128)(2,1)} %bitcast.14, bf16[16,128,128]{2,1,0:T(8,128)(2,1)S(1)} %get-tuple-element.8.mid_ref), custom_call_target="tpu_custom_call" | custom-call | flops 600000000 | bytes 6291456 | tf_op jit(solution)/shard_map/pallas_call | solution.py:272
  59.5 0.0 copy-start.1
  59.6 4.0 %shard_map.85.part1_ref = f32[512,1024]{1,0:T(8,128)S(1)} custom-call(f32[16]{0:T(128)} %rate_ref.9, s32[1,512]{1,0:T(1,128)} %u_ref.9, bf16[512,2048]{1,0:T(8,128)(2,1)} %bitcast.8, bf16[512,2048]{1,0:T(8,128)(2,1)} %bitcast.12, bf16[512,2048]{1,0:T(8,128)(2,1)} %bitcast.15, bf16[16,128,128]{2,1,0:T(8,128)(2,1)S(1)} %get-tuple-element.8.mid_ref), custom_call_target="tpu_custom_call" | custom-call | flops 600000000 | bytes 6291456 | tf_op jit(solution)/shard_map/pallas_call | solution.py:272
  63.6 0.0 copy-done.1
  63.6 6.6 %shard_map.86.g_ref = bf16[512,2048]{1,0:T(8,128)(2,1)S(1)} custom-call(f32[16]{0:T(128)} %rate_ref.9, s32[1,512]{1,0:T(1,128)} %u_ref.9, bf16[2064,128]{1,0:T(8,128)(2,1)S(1)} %collective-permute-done.one_ref, bf16[2064,128]{1,0:T(8,128)(2,1)S(1)} %collective-permute-done.1.two_ref, bf16[512,2048]{1,0:T(8,128)(2,1)} %bitcast.9, ...), custom_call_target="tpu_custom_call" | custom-call | flops 300000000 | bytes 11534336 | tf_op jit(solution)/shard_map/pallas_call | solution.py:283
  70.2 3.9 %shard_map.87.refs_8_ = bf16[512,2048]{1,0:T(8,128)(2,1)} custom-call(bf16[512,2048]{1,0:T(8,128)(2,1)S(1)} %shard_map.86.g_ref, bf16[256,1024]{1,0:T(8,128)(2,1)S(1)} %pad_maximum_fusion.refs_0_, bf16[256,1024]{1,0:T(8,128)(2,1)S(1)} %constant_dynamic-update-slice_fusion.refs_1_, bf16[256,1024]{1,0:T(8,128)(2,1)S(1)} %collective-permute-done.11.refs_2_, ...), custom_call_target="tpu_custom_call" | custom-call | flops 2150000128 | bytes 7340032 | tf_op jit(solution)/shard_map/pallas_call | solution.py:299
  74.1 0.0 collective-permute-done.16.refs_4_
  74.1 0.0 collective-permute-done.14.refs_3_
  74.1 0.0 collective-permute-done.18.refs_5_
  74.1 0.0 collective-permute-done.20.refs_6_
  74.1 0.0 collective-permute-done.22.refs_7_
  74.1 3.9 %shard_map.88 = bf16[512,2048]{1,0:T(8,128)(2,1)} custom-call(bf16[512,2048]{1,0:T(8,128)(2,1)S(1)} %shard_map.86.g_ref, bf16[256,1024]{1,0:T(8,128)(2,1)S(1)} %collective-permute-done.5.refs_0_, bf16[256,1024]{1,0:T(8,128)(2,1)S(1)} %collective-permute-done.10.refs_1_, ...), custom_call_target="tpu_custom_call", output_to_operand_aliasing={{}: (9, {})} | custom-call | flops 2150000128 | bytes 7340032 | tf_op jit(solution)/shard_map/pallas_call | solution.py:299
  (6 shorter events, 0.1 us)
Async XLA Ops:
  0.0 1.0 %copy-start = (bf16[64,2048]{1,0:T(8,128)(2,1)S(1)}, bf16[64,2048]{1,0:T(8,128)(2,1)}, u32[]{:S(2)}) copy-start(bf16[64,2048]{1,0:T(8,128)(2,1)} %param.15) | copy-start | bytes 786436
  1.0 9.1 %collective-permute-start.2 = (bf16[64,1024]{1,0:T(8,128)(2,1)S(1)}, bf16[64,1024]{1,0:T(8,128)(2,1)S(1)}, u32[]{:S(2)}, u32[]{:S(2)}) collective-permute-start(bf16[64,1024]{1,0:T(8,128)(2,1)S(1)} %constant_dynamic-slice_fusion), channel_id=1, source_target_pairs={{0,64},{1,9},{2,66},{3,11},{4,68},{5,13},{6,70},{7,15},{8,72},{9,1... | collective-permute-start | bytes 393224 | tf_op jit(solution)/shard_map/ppermute | solution.py:195
  3.5 6.5 %collective-permute-start.3 = (bf16[64,1024]{1,0:T(8,128)(2,1)S(1)}, bf16[64,1024]{1,0:T(8,128)(2,1)S(1)}, u32[]{:S(2)}, u32[]{:S(2)}) collective-permute-start(bf16[64,1024]{1,0:T(8,128)(2,1)S(1)} %constant_dynamic-slice_fusion), channel_id=1, source_target_pairs={{0,32},{1,57},{2,34},{3,59},{4,36},{5,61},{6,38},{7,63},{8,40},{9,... | collective-permute-start | bytes 393224 | tf_op jit(solution)/shard_map/ppermute | solution.py:195
  10.0 6.3 %collective-permute-start.6 = (bf16[64,1024]{1,0:T(8,128)(2,1)S(1)}, bf16[64,1024]{1,0:T(8,128)(2,1)S(1)}, u32[]{:S(2)}, u32[]{:S(2)}) collective-permute-start(bf16[64,1024]{1,0:T(8,128)(2,1)S(1)} %collective-permute-done.2), channel_id=1, source_target_pairs={{0,64},{1,9},{2,66},{3,11},{4,68},{5,13},{6,70},{7,15},{8,72},{9,1... | collective-permute-start | bytes 393224 | tf_op jit(solution)/shard_map/ppermute | solution.py:195
  10.0 15.1 %collective-permute-start.4 = (bf16[64,1024]{1,0:T(8,128)(2,1)S(1)}, bf16[64,1024]{1,0:T(8,128)(2,1)S(1)}, u32[]{:S(2)}, u32[]{:S(2)}) collective-permute-start(bf16[64,1024]{1,0:T(8,128)(2,1)S(1)} %collective-permute-done.3), channel_id=1, source_target_pairs={{0,64},{1,57},{2,66},{3,59},{4,68},{5,61},{6,70},{7,63},{8,72},{9,... | collective-permute-start | bytes 393224 | tf_op jit(solution)/shard_map/ppermute | solution.py:195
  16.3 13.1 %collective-permute-start.7 = (bf16[64,1024]{1,0:T(8,128)(2,1)S(1)}, bf16[64,1024]{1,0:T(8,128)(2,1)S(1)}, u32[]{:S(2)}, u32[]{:S(2)}) collective-permute-start(bf16[64,1024]{1,0:T(8,128)(2,1)S(1)} %collective-permute-done.6), channel_id=1, source_target_pairs={{0,64},{1,9},{2,66},{3,11},{4,68},{5,13},{6,70},{7,15},{8,72},{9,1... | collective-permute-start | bytes 393224 | tf_op jit(solution)/shard_map/ppermute | solution.py:195
  20.3 17.5 %collective-permute-start = (bf16[2064,128]{1,0:T(8,128)(2,1)S(1)}, bf16[2064,128]{1,0:T(8,128)(2,1)S(1)}, u32[]{:S(2)}, u32[]{:S(2)}) collective-permute-start(bf16[2064,128]{1,0:T(8,128)(2,1)S(1)} %get-tuple-element.7.own_ref), channel_id=1, source_target_pairs={{0,1},{1,2},{2,3},{3,4},{4,5},{5,6},{6,7},{8,9},{9,10},{10,11},{11... | collective-permute-start | bytes 1585160 | tf_op jit(solution)/shard_map/ppermute | solution.py:262
  25.2 7.2 %collective-permute-start.8 = (bf16[64,1024]{1,0:T(8,128)(2,1)S(1)}, bf16[64,1024]{1,0:T(8,128)(2,1)S(1)}, u32[]{:S(2)}, u32[]{:S(2)}) collective-permute-start(bf16[64,1024]{1,0:T(8,128)(2,1)S(1)} %collective-permute-done.4), channel_id=1, source_target_pairs={{0,64},{1,57},{2,66},{3,59},{4,68},{5,61},{6,70},{7,63},{8,72},{9,... | collective-permute-start | bytes 393224 | tf_op jit(solution)/shard_map/ppermute | solution.py:195
  29.5 6.8 %collective-permute-start.9 = (bf16[64,1024]{1,0:T(8,128)(2,1)S(1)}, bf16[64,1024]{1,0:T(8,128)(2,1)S(1)}, u32[]{:S(2)}, u32[]{:S(2)}) collective-permute-start(bf16[64,1024]{1,0:T(8,128)(2,1)S(1)} %get-tuple-element.9), channel_id=1, source_target_pairs={{0,192},{1,9},{2,194},{3,11},{4,196},{5,13},{6,198},{7,15},{8,200}... | collective-permute-start | bytes 393224 | tf_op jit(solution)/shard_map/ppermute | solution.py:195
  29.6 9.6 %collective-permute-start.11 = (bf16[256,1024]{1,0:T(8,128)(2,1)S(1)}, bf16[256,1024]{1,0:T(8,128)(2,1)S(1)}, u32[]{:S(2)}, u32[]{:S(2)}) collective-permute-start(bf16[256,1024]{1,0:T(8,128)(2,1)S(1)} %pad_maximum_fusion.refs_0_), channel_id=1, source_target_pairs={{0,8},{1,65},{2,10},{3,67},{4,12},{5,69},{6,14},{7,71},{8,16},{9,7... | collective-permute-start | bytes 1572872 | tf_op jit(solution)/shard_map/ppermute | solution.py:195
  29.7 12.7 %collective-permute-start.15 = (bf16[256,1024]{1,0:T(8,128)(2,1)S(1)}, bf16[256,1024]{1,0:T(8,128)(2,1)S(1)}, u32[]{:S(2)}, u32[]{:S(2)}) collective-permute-start(bf16[256,1024]{1,0:T(8,128)(2,1)S(1)} %pad_maximum_fusion.refs_0_), channel_id=1, source_target_pairs={{0,56},{1,193},{2,58},{3,195},{4,60},{5,197},{6,62},{7,199},{8,0},... | collective-permute-start | bytes 1572872 | tf_op jit(solution)/shard_map/ppermute | solution.py:195
  32.4 11.8 %collective-permute-start.5 = (bf16[256,1024]{1,0:T(8,128)(2,1)S(1)}, bf16[256,1024]{1,0:T(8,128)(2,1)S(1)}, u32[]{:S(2)}, u32[]{:S(2)}) collective-permute-start(bf16[256,1024]{1,0:T(8,128)(2,1)S(1)} %pad_maximum_fusion.refs_0_), channel_id=1, source_target_pairs={{0,1},{1,0},{2,3},{3,2},{4,5},{5,4},{6,7},{7,6},{8,9},{9,8},{10,11... | collective-permute-start | bytes 1572872 | tf_op jit(solution)/shard_map/ppermute | solution.py:199
  36.3 8.4 %collective-permute-start.17 = (bf16[256,1024]{1,0:T(8,128)(2,1)S(1)}, bf16[256,1024]{1,0:T(8,128)(2,1)S(1)}, u32[]{:S(2)}, u32[]{:S(2)}) collective-permute-start(bf16[256,1024]{1,0:T(8,128)(2,1)S(1)} %constant_dynamic-update-slice_fusion.refs_1_), channel_id=1, source_target_pairs={{0,56},{1,193},{2,58},{3,195},{4,60},{5,197},{6,62},{7,199},{8,0},... | collective-permute-start | bytes 1572872 | tf_op jit(solution)/shard_map/ppermute | solution.py:195
  37.9 9.2 %collective-permute-start.13 = (bf16[256,1024]{1,0:T(8,128)(2,1)S(1)}, bf16[256,1024]{1,0:T(8,128)(2,1)S(1)}, u32[]{:S(2)}, u32[]{:S(2)}) collective-permute-start(bf16[256,1024]{1,0:T(8,128)(2,1)S(1)} %constant_dynamic-update-slice_fusion.refs_1_), channel_id=1, source_target_pairs={{0,8},{1,65},{2,10},{3,67},{4,12},{5,69},{6,14},{7,71},{8,16},{9,7... | collective-permute-start | bytes 1572872 | tf_op jit(solution)/shard_map/ppermute | solution.py:195
  39.3 13.0 %collective-permute-start.1 = (bf16[2064,128]{1,0:T(8,128)(2,1)S(1)}, bf16[2064,128]{1,0:T(8,128)(2,1)S(1)}, u32[]{:S(2)}, u32[]{:S(2)}) collective-permute-start(bf16[2064,128]{1,0:T(8,128)(2,1)S(1)} %shard_map.83), channel_id=1, source_target_pairs={{0,2},{1,3},{2,4},{3,5},{4,6},{5,7},{8,10},{9,11},{10,12},{11,13},... | collective-permute-start | bytes 1585160 | tf_op jit(solution)/shard_map/ppermute | solution.py:282
  42.4 5.0 %collective-permute-start.10 = (bf16[256,1024]{1,0:T(8,128)(2,1)S(1)}, bf16[256,1024]{1,0:T(8,128)(2,1)S(1)}, u32[]{:S(2)}, u32[]{:S(2)}) collective-permute-start(bf16[256,1024]{1,0:T(8,128)(2,1)S(1)} %constant_dynamic-update-slice_fusion.refs_1_), channel_id=1, source_target_pairs={{0,1},{1,0},{2,3},{3,2},{4,5},{5,4},{6,7},{7,6},{8,9},{9,8},{10,11... | collective-permute-start | bytes 1572872 | tf_op jit(solution)/shard_map/ppermute | solution.py:199
  44.2 10.4 %collective-permute-start.19 = (bf16[256,1024]{1,0:T(8,128)(2,1)S(1)}, bf16[256,1024]{1,0:T(8,128)(2,1)S(1)}, u32[]{:S(2)}, u32[]{:S(2)}) collective-permute-start(bf16[256,1024]{1,0:T(8,128)(2,1)S(1)} %collective-permute-done.11.refs_2_), channel_id=1, source_target_pairs={{0,8},{1,65},{2,10},{3,67},{4,12},{5,69},{6,14},{7,71},{8,16},{9,7... | collective-permute-start | bytes 1572872 | tf_op jit(solution)/shard_map/ppermute | solution.py:195
  44.7 10.0 %collective-permute-start.12 = (bf16[256,1024]{1,0:T(8,128)(2,1)S(1)}, bf16[256,1024]{1,0:T(8,128)(2,1)S(1)}, u32[]{:S(2)}, u32[]{:S(2)}) collective-permute-start(bf16[256,1024]{1,0:T(8,128)(2,1)S(1)} %collective-permute-done.11.refs_2_), channel_id=1, source_target_pairs={{0,1},{1,0},{2,3},{3,2},{4,5},{5,4},{6,7},{7,6},{8,9},{9,8},{10,11... | collective-permute-start | bytes 1572872 | tf_op jit(solution)/shard_map/ppermute | solution.py:199
  47.1 8.0 %collective-permute-start.21 = (bf16[256,1024]{1,0:T(8,128)(2,1)S(1)}, bf16[256,1024]{1,0:T(8,128)(2,1)S(1)}, u32[]{:S(2)}, u32[]{:S(2)}) collective-permute-start(bf16[256,1024]{1,0:T(8,128)(2,1)S(1)} %collective-permute-done.17.refs_5_), channel_id=1, source_target_pairs={{0,56},{1,193},{2,58},{3,195},{4,60},{5,197},{6,62},{7,199},{8,0},... | collective-permute-start | bytes 1572872 | tf_op jit(solution)/shard_map/ppermute | solution.py:195
  47.4 26.7 %collective-permute-start.16 = (bf16[256,1024]{1,0:T(8,128)(2,1)S(1)}, bf16[256,1024]{1,0:T(8,128)(2,1)S(1)}, u32[]{:S(2)}, u32[]{:S(2)}) collective-permute-start(bf16[256,1024]{1,0:T(8,128)(2,1)S(1)} %collective-permute-done.15.refs_4_), channel_id=1, source_target_pairs={{0,1},{1,0},{2,3},{3,2},{4,5},{5,4},{6,7},{7,6},{8,9},{9,8},{10,11... | collective-permute-start | bytes 1572872 | tf_op jit(solution)/shard_map/ppermute | solution.py:199
  52.3 21.8 %collective-permute-start.18 = (bf16[256,1024]{1,0:T(8,128)(2,1)S(1)}, bf16[256,1024]{1,0:T(8,128)(2,1)S(1)}, u32[]{:S(2)}, u32[]{:S(2)}) collective-permute-start(bf16[256,1024]{1,0:T(8,128)(2,1)S(1)} %collective-permute-done.17.refs_5_), channel_id=1, source_target_pairs={{0,1},{1,0},{2,3},{3,2},{4,5},{5,4},{6,7},{7,6},{8,9},{9,8},{10,11... | collective-permute-start | bytes 1572872 | tf_op jit(solution)/shard_map/ppermute | solution.py:199
  54.6 19.5 %collective-permute-start.14 = (bf16[256,1024]{1,0:T(8,128)(2,1)S(1)}, bf16[256,1024]{1,0:T(8,128)(2,1)S(1)}, u32[]{:S(2)}, u32[]{:S(2)}) collective-permute-start(bf16[256,1024]{1,0:T(8,128)(2,1)S(1)} %collective-permute-done.13.refs_3_), channel_id=1, source_target_pairs={{0,1},{1,0},{2,3},{3,2},{4,5},{5,4},{6,7},{7,6},{8,9},{9,8},{10,11... | collective-permute-start | bytes 1572872 | tf_op jit(solution)/shard_map/ppermute | solution.py:199
  54.7 19.4 %collective-permute-start.20 = (bf16[256,1024]{1,0:T(8,128)(2,1)S(1)}, bf16[256,1024]{1,0:T(8,128)(2,1)S(1)}, u32[]{:S(2)}, u32[]{:S(2)}) collective-permute-start(bf16[256,1024]{1,0:T(8,128)(2,1)S(1)} %collective-permute-done.19.refs_6_), channel_id=1, source_target_pairs={{0,1},{1,0},{2,3},{3,2},{4,5},{5,4},{6,7},{7,6},{8,9},{9,8},{10,11... | collective-permute-start | bytes 1572872 | tf_op jit(solution)/shard_map/ppermute | solution.py:199
  55.2 18.9 %collective-permute-start.22 = (bf16[256,1024]{1,0:T(8,128)(2,1)S(1)}, bf16[256,1024]{1,0:T(8,128)(2,1)S(1)}, u32[]{:S(2)}, u32[]{:S(2)}) collective-permute-start(bf16[256,1024]{1,0:T(8,128)(2,1)S(1)} %collective-permute-done.21.refs_7_), channel_id=1, source_target_pairs={{0,1},{1,0},{2,3},{3,2},{4,5},{5,4},{6,7},{7,6},{8,9},{9,8},{10,11... | collective-permute-start | bytes 1572872 | tf_op jit(solution)/shard_map/ppermute | solution.py:199
  59.5 4.0 %copy-start.1 = (f32[2048]{0:T(1024)S(1)}, f32[2048]{0:T(1024)}, u32[]{:S(2)}) copy-start(f32[2048]{0:T(1024)} %param.14) | copy-start | bytes 24580
